TPU v7x, 32 devices: a whole 2x2x4 slice. The times are simulated.
32 devices in a mesh: parts: 2 (over y), req: 8 (over z, x), tp: 2 (over core).
Axes of the slice: x: 2, y: 2, z: 4, core: 2. Of those that a mesh axis runs over, the one named last changes fastest.
Arguments:
- counts: int32 [16], P('parts'), parts along dimension 0, may hold values from 1 to 2, as said below
- move_plan: int32 [32], P('parts'), parts along dimension 0, may hold values from 0 to 15, as said below
- ssm_state: float32 [32, 128, 4096], P(('parts', 'req'), 'tp'), parts along dimension 0, may hold values from -6 to 6
- conv_x_state: bfloat16 [32, 3, 8192], P(('parts', 'req'), None, 'tp'), parts along dimension 0, may hold values from -6 to 6
- conv_bc_state: bfloat16 [32, 3, 4, 128], P(('parts', 'req'), None, 'tp'), parts along dimension 0, may hold values from -6 to 6
- x_in: bfloat16 [32, 4, 8192], P(('parts', 'req'), None, 'tp'), parts along dimension 0, may hold values from -6 to 6
- bc_in: bfloat16 [32, 4, 4, 128], P(('parts', 'req'), None, 'tp'), parts along dimension 0, may hold values from -6 to 6
- z_in: bfloat16 [32, 4, 8192], P(('parts', 'req'), None, 'tp'), parts along dimension 0, may hold values from -6 to 6
- dt_in: float32 [32, 4, 128], P(('parts', 'req'), None, 'tp'), parts along dimension 0, may hold values from -1.5 to 1.5
- conv_w_x: float32 [4, 8192], P(None, 'tp'), may hold values from -3 to 3
- conv_b_x: float32 [8192], P('tp'), may hold values from -3 to 3
- conv_w_bc: float32 [4, 4, 128], P(None, 'tp'), may hold values from -3 to 3
- conv_b_bc: float32 [4, 128], P('tp'), may hold values from -3 to 3
- dt_bias: float32 [128], P('tp'), may hold values from -4 to -1
- a_log: float32 [128], P('tp'), may hold values from -2.5 to -0.5
- d_skip: float32 [128], P('tp'), may hold values from 0.3 to 1.5
- norm_w: float32 [8192], P('tp'), may hold values from 0.1 to 1.9
Outputs:
- y_out: bfloat16 [32, 4, 8192], P(('parts', 'req'), None, 'tp'), parts along dimension 0
- new_ssm: float32 [32, 128, 4096], P(('parts', 'req'), 'tp'), parts along dimension 0
- new_conv_x: bfloat16 [32, 3, 8192], P(('parts', 'req'), None, 'tp'), parts along dimension 0
- new_conv_bc: bfloat16 [32, 3, 4, 128], P(('parts', 'req'), None, 'tp'), parts along dimension 0
There are 2 independent parts, one for each index of `parts`. A program takes and returns all parts, laid end to end along the dimension named above; an argument that names none is the same for every part. Nothing has to cross between parts.
Inputs may be any that keep to these rules, and one draw needn't show every extreme that they name: `counts`: at least 1; every draw has owners with 2 live requests. `move_plan`: A destination slot is owner times 2 plus a local slot. Entries of slots that are not live are meaningless. Live requests have distinct destinations. An owner sends at most 1 live requests to other owners and receives at most 1 from other owners, and keeps at most 1 of its own; both bounds are reached in every draw, and some owner has all 2 destination slots taken.
All inputs are finite; a program needn't handle non-finite values.
Results may differ from a plain program's by a relative error of at most 0.001.
Values may be sent and summed in bfloat16 or wider, within the bound.
A program may use at most 128 MiB of HBM per device.

v0:
```python
import jax
import jax.numpy as jnp
from jax import lax
from jax.sharding import PartitionSpec as P

H = 128
P_SIZE = 64


def on_device(
    counts,
    move_plan,
    ssm_state,
    conv_x_state,
    conv_bc_state,
    x_in,
    bc_in,
    z_in,
    dt_in,
    conv_w_x,
    conv_b_x,
    conv_w_bc,
    conv_b_bc,
    dt_bias,
    a_log,
    d_skip,
    norm_w,
):
    owners = lax.axis_size("req")
    owner = lax.axis_index("req")
    slots, heads_loc, columns = ssm_state.shape
    places, steps, channels = x_in.shape
    groups_loc = conv_bc_state.shape[2]
    pair = conv_bc_state.shape[3]
    state_size = pair // 2
    head_dim = channels // heads_loc
    reqs = move_plan.shape[0]
    ids = jnp.arange(reqs, dtype=jnp.int32)
    home = ids // slots
    live = ids % slots < jnp.take(counts, home)
    conv_flat = jnp.concatenate(
        [conv_x_state.reshape(slots, -1), conv_bc_state.reshape(slots, -1)], 1
    )
    conv_width = conv_flat.shape[1]
    zero_conv = jnp.zeros((), jnp.bfloat16)
    spread_state = lax.all_to_all(
        ssm_state.reshape(slots, owners, -1), "req", split_axis=1, concat_axis=0, tiled=True
    )
    spread_conv = lax.all_to_all(
        conv_flat.reshape(slots, owners, -1), "req", split_axis=1, concat_axis=0, tiled=True
    )
    targets = jnp.arange(owners * places, dtype=jnp.int32)
    match = live[None, :] & (move_plan[None, :] == targets[:, None])
    source = jnp.sum(jnp.where(match, ids[None, :], 0), axis=1)
    hit = jnp.any(match, axis=1)
    keep = hit.astype(jnp.float32)
    picked_state = jnp.take(spread_state, source, axis=0) * keep[:, None, None]
    picked_conv = jnp.where(hit[:, None, None], jnp.take(spread_conv, source, axis=0), zero_conv)
    arrived_state = lax.all_to_all(picked_state, "req", split_axis=0, concat_axis=1, tiled=True)
    arrived_conv = lax.all_to_all(picked_conv, "req", split_axis=0, concat_axis=1, tiled=True)
    state = arrived_state.reshape(places, heads_loc, columns)
    conv = arrived_conv.reshape(places, conv_width)
    mask = lax.dynamic_slice_in_dim(keep, owner * places, places)
    conv_x = conv[:, : 3 * channels].reshape(places, 3, channels)
    conv_bc = conv[:, 3 * channels :].reshape(places, 3, groups_loc, pair)
    per_group = heads_loc // groups_loc
    rate = jnp.exp(a_log)
    status = state.reshape(places, heads_loc, head_dim, state_size)
    scaling = 1.0 / (H * P_SIZE)
    outputs = []
    for step in range(steps):
        x_new = x_in[:, step]
        window = jnp.concatenate([conv_x, x_new[:, None]], 1).astype(jnp.float32)
        xconv = jax.nn.silu(jnp.sum(window * conv_w_x[None], axis=1) + conv_b_x)
        conv_x = jnp.concatenate([conv_x[:, 1:], x_new[:, None]], 1)
        bc_new = bc_in[:, step]
        bwindow = jnp.concatenate([conv_bc, bc_new[:, None]], 1).astype(jnp.float32)
        bconv = jax.nn.silu(jnp.sum(bwindow * conv_w_bc[None], axis=1) + conv_b_bc)
        conv_bc = jnp.concatenate([conv_bc[:, 1:], bc_new[:, None]], 1)
        b_head = jnp.repeat(bconv[..., :state_size], per_group, axis=1)
        c_head = jnp.repeat(bconv[..., state_size:], per_group, axis=1)
        delta = jax.nn.softplus(dt_in[:, step] + dt_bias)
        decay = jnp.exp(-delta * rate)
        heads_x = xconv.reshape(places, heads_loc, head_dim)
        status = (
            decay[:, :, None, None] * status
            + (delta[:, :, None] * heads_x)[..., None] * b_head[:, :, None, :]
        )
        mixed = jnp.sum(status * c_head[:, :, None, :], axis=-1) + d_skip[None, :, None] * heads_x
        gated = mixed.reshape(places, channels) * jax.nn.silu(z_in[:, step].astype(jnp.float32))
        total = lax.psum(jnp.sum(gated * gated, axis=-1), "tp")
        outputs.append(gated * lax.rsqrt(total * scaling + 1e-05)[:, None] * norm_w)
    normed = jnp.stack(outputs, 1)
    y_out = (normed * mask[:, None, None]).astype(jnp.bfloat16)
    new_ssm = status.reshape(places, heads_loc, columns) * mask[:, None, None]
    filled = mask > 0.5
    new_conv_x = jnp.where(filled[:, None, None], conv_x, jnp.zeros_like(conv_x))
    new_conv_bc = jnp.where(filled[:, None, None, None], conv_bc, jnp.zeros_like(conv_bc))
    return (y_out, new_ssm, new_conv_x, new_conv_bc)


def solution(mesh):
    in_specs = (
        P("parts"),
        P("parts"),
        P(("parts", "req"), "tp", None),
        P(("parts", "req"), None, "tp"),
        P(("parts", "req"), None, "tp", None),
        P(("parts", "req"), None, "tp"),
        P(("parts", "req"), None, "tp", None),
        P(("parts", "req"), None, "tp"),
        P(("parts", "req"), None, "tp"),
        P(None, "tp"),
        P("tp"),
        P(None, "tp", None),
        P("tp", None),
        P("tp"),
        P("tp"),
        P("tp"),
        P("tp"),
    )
    out_specs = (
        P(("parts", "req"), None, "tp"),
        P(("parts", "req"), "tp", None),
        P(("parts", "req"), None, "tp"),
        P(("parts", "req"), None, "tp", None),
    )
    return jax.shard_map(
        on_device, mesh=mesh, in_specs=in_specs, out_specs=out_specs, check_vma=False
    )
```

profile of v0, /device:TPU:0, one launch (start us, length us, event | category | flops | bytes accessed | tf_op | source)
XLA Modules:
  0.0 195.3 jit_solution(5956617972472375227)
XLA Ops:
  0.6 0.7 reshape.1063
  1.4 0.8 pad_maximum_fusion.1
  3.0 7.3 %all-to-all-start.2 = ((bf16[2,8,1632]{2,0,1:T(2,128)(2,1)}), bf16[2,8,1632]{2,0,1:T(2,128)(2,1)S(1)}, u32[]{:S(2)}, u32[]{:S(2)}) async-start(bf16[2,8,1632]{2,0,1:T(2,128)(2,1)} %copy.107), calls=%async_computation.2 | async-start | bytes 106496 | tf_op jit(solution)/shard_map/all_to_all | solution.py:49
  11.0 0.8 select_reduce_fusion
  11.8 0.8 fusion.46
  12.6 4.5 %all-to-all-done.2 = bf16[2,8,1632]{2,0,1:T(2,128)(2,1)S(1)} async-done(((bf16[2,8,1632]{2,0,1:T(2,128)(2,1)}), bf16[2,8,1632]{2,0,1:T(2,128)(2,1)S(1)}, u32[]{:S(2)}, u32[]{:S(2)}) %all-to-all-start.2) | async-done | bytes 52256 | tf_op jit(solution)/shard_map/all_to_all | solution.py:49
  19.7 3.3 %all-to-all-start.3 = ((bf16[8,2,1632]{2,1,0:T(2,128)(2,1)}), bf16[8,2,1632]{2,1,0:T(2,128)(2,1)S(1)}, u32[]{:S(2)}, u32[]{:S(2)}) async-start(bf16[8,2,1632]{2,1,0:T(2,128)(2,1)} %reshape.1103), calls=%async_computation.3 | async-start | bytes 106496 | tf_op jit(solution)/shard_map/all_to_all | solution.py:60
  23.1 1.8 reshape.1061
  24.8 2.9 %copy.104 = f32[2,8,32768]{2,0,1:T(2,128)} copy(f32[2,8,32768]{2,1,0:T(8,128)S(1)} %reshape.1061) | data formatting | bytes 4194304 | tf_op jit(solution)/shard_map/reshape | solution.py:47
  27.8 2.0 %all-to-all-done.3 = bf16[8,2,1632]{2,1,0:T(2,128)(2,1)S(1)} async-done(((bf16[8,2,1632]{2,1,0:T(2,128)(2,1)}), bf16[8,2,1632]{2,1,0:T(2,128)(2,1)S(1)}, u32[]{:S(2)}, u32[]{:S(2)}) %all-to-all-start.3) | async-done | bytes 52256 | tf_op jit(solution)/shard_map/all_to_all | solution.py:60
  29.8 4.1 %all-to-all-start = ((f32[2,8,32768]{2,0,1:T(2,128)}), f32[2,8,32768]{2,0,1:T(2,128)S(1)}, u32[]{:S(2)}, u32[]{:S(2)}) async-start(f32[2,8,32768]{2,0,1:T(2,128)} %copy.104), calls=%async_computation | async-start | bytes 4194304 | tf_op jit(solution)/shard_map/all_to_all | solution.py:46
  35.4 45.1 %all-to-all-done = f32[2,8,32768]{2,0,1:T(2,128)S(1)} async-done(((f32[2,8,32768]{2,0,1:T(2,128)}), f32[2,8,32768]{2,0,1:T(2,128)S(1)}, u32[]{:S(2)}, u32[]{:S(2)}) %all-to-all-start) | async-done | bytes 2097184 | tf_op jit(solution)/shard_map/all_to_all | solution.py:46
  80.5 1.3 copy-done.2
  81.9 2.7 %reshape.1080 = f32[16,32768]{1,0:T(8,128)S(1)} reshape(f32[8,2,1,32768]{3,1,0,2:T(2,128)} %bitcast.161) | data formatting | bytes 4194304 | tf_op jit(solution)/shard_map/all_to_all | solution.py:46
  84.6 2.4 %gather_fusion.1 = f32[16,32768]{1,0:T(8,128)} fusion(f32[16,32768]{1,0:T(8,128)S(1)} %reshape.1080, s32[1024]{0:T(1024)S(1)} %pad_clamp_fusion), kind=kCustom, calls=%fused_computation.1 | custom fusion | bytes 4194368 | tf_op jit(solution)/shard_map/jit(_take)/gather | solution.py:57
  87.0 1.8 fusion
  88.8 3.5 %copy.105 = f32[16,1,32768]{2,1,0:T(1,128)} copy(f32[16,1,32768]{2,0,1:T(8,128)S(1)} %fusion) | data formatting | bytes 4194304 | tf_op jit(solution)/shard_map/mul | solution.py:57
  92.3 3.9 %all-to-all-start.1 = ((f32[16,1,32768]{2,1,0:T(1,128)}), f32[16,1,32768]{2,1,0:T(1,128)S(1)}, u32[]{:S(2)}, u32[]{:S(2)}) async-start(f32[16,1,32768]{2,1,0:T(1,128)} %copy.105), calls=%async_computation.1 | async-start | bytes 4194304 | tf_op jit(solution)/shard_map/all_to_all | solution.py:59
  97.5 0.7 copy.115
  99.4 45.0 %all-to-all-done.1 = f32[16,1,32768]{2,1,0:T(1,128)S(1)} async-done(((f32[16,1,32768]{2,1,0:T(1,128)}), f32[16,1,32768]{2,1,0:T(1,128)S(1)}, u32[]{:S(2)}, u32[]{:S(2)}) %all-to-all-start.1) | async-done | bytes 2097184 | tf_op jit(solution)/shard_map/all_to_all | solution.py:59
  144.4 1.3 copy-done.1
  145.7 2.8 %copy.130 = f32[8,2,1,32768]{3,0,1,2:T(8,128)S(1)} copy(f32[8,2,1,32768]{3,2,1,0:T(1,128)} %bitcast.160) | data formatting | bytes 4194304 | tf_op jit(solution)/shard_map/all_to_all | solution.py:59
  148.5 3.0 %reshape_reshape.5 = f32[2,64,64,64]{3,2,1,0:T(8,128)} reshape(f32[2,8,1,32768]{3,1,0,2:T(8,128)S(1)} %bitcast.158) | data formatting | bytes 4194304 | tf_op jit(solution)/shard_map/reshape;reshape | solution.py:68
  151.7 13.2 %multiply_reduce_fusion.1 = (f32[2,64,64]{2,1,0:T(8,128)S(1)}, f32[2,64,64]{2,1,0:T(8,128)S(1)}, f32[2,64,64]{2,1,0:T(8,128)S(1)}, f32[2,64,64]{2,1,0:T(8,128)S(...) fusion(f32[2,64,64]{2,1,0:T(8,128)S(1)} %bitcast.162, ...), kind=kLoop, calls=%fused_computation.4 | loop fusion | flops 10452992 | bytes 11012096 | tf_op jit(solution)/shard_map/reduce_sum | solution.py:89
  165.7 1.6 reshape_reshape.6
  167.7 2.5 %all-reduce = (f32[2]{0:T(128)S(1)}, f32[2]{0:T(128)S(1)}, f32[2]{0:T(128)S(1)}, f32[2]{0:T(128)S(1)}) all-reduce(f32[2]{0:T(128)S(1)} %get-tuple-element.35, f32[2]{0:T(128)S(1)} %get-tuple-element.34, f32[2]{0:T(128)S(1)} %get-tuple-element.33, f32[2]{0:T(128)S(1)} %get-tuple-element.32), channel_id=1, replica_groups=mesh['parts'=2,'req'=8,'tp'=2] {'tp'}, use_global_device_ids=true, to_apply=%region_21.22 | all-reduce | flops 8 | bytes 64 | tf_op jit(solution)/shard_map/psum | solution.py:91
  170.7 0.7 copy.114
  171.4 3.5 %mul.869 = f32[2,64,4096]{2,1,0:T(8,128)S(1)} reshape(f32[2,64,64,64]{3,2,1,0:T(8,128)} %get-tuple-element.57) | data formatting | bytes 4194304 | tf_op jit(solution)/shard_map/mul | solution.py:87
  174.9 4.8 %mul.867 = f32[2,64,4096]{2,1,0:T(8,128)} reshape(f32[2,64,64,64]{3,2,1,0:T(8,128)} %get-tuple-element.56) | data formatting | bytes 4194304 | tf_op jit(solution)/shard_map/mul | solution.py:87
  179.7 4.8 %mul.865 = f32[2,64,4096]{2,1,0:T(8,128)} reshape(f32[2,64,64,64]{3,2,1,0:T(8,128)} %get-tuple-element.55) | data formatting | bytes 4194304 | tf_op jit(solution)/shard_map/mul | solution.py:87
  184.4 4.8 %mul.863 = f32[2,64,4096]{2,1,0:T(8,128)} reshape(f32[2,64,64,64]{3,2,1,0:T(8,128)} %get-tuple-element.54) | data formatting | bytes 4194304 | tf_op jit(solution)/shard_map/mul | solution.py:87
  189.2 6.1 %add_multiply_fusion = f32[2,64,4096]{2,1,0:T(8,128)} fusion(f32[2,64,4096]{2,1,0:T(8,128)S(1)} %mul.869, f32[2,64,4096]{2,1,0:T(8,128)} %mul.867, f32[2,64,4096]{2,1,0:T(8,128)} %mul.865, f32[2,64,4096]{2,1,0:T(8,128)} %mul.863, f32[2,64,4096]{2,1,0:T(8,128)} %reshape_reshape.6, f32[2]{0:T(128)S(1)} %get-tuple-element.45, ...), kind=kLoop, calls=%fused_computation.13 | loop fusion | flops 4718592 | bytes 12584968 | tf_op jit(solution)/shard_map/mul | solution.py:95
  (106 shorter events, 9.7 us)
Async XLA Ops:
  0.6 9.7 %copy-start = (s32[8]{0:T(128)S(1)}, s32[8]{0:T(128)}, u32[]{:S(2)}) copy-start(s32[8]{0:T(128)} %param.17) | copy-start | bytes 100
  3.0 14.1 %all-to-all-start.2 = ((bf16[2,8,1632]{2,0,1:T(2,128)(2,1)}), bf16[2,8,1632]{2,0,1:T(2,128)(2,1)S(1)}, u32[]{:S(2)}, u32[]{:S(2)}) async-start(bf16[2,8,1632]{2,0,1:T(2,128)(2,1)} %copy.107), calls=%async_computation.2 | async-start | bytes 106496 | tf_op jit(solution)/shard_map/all_to_all | solution.py:49
  19.7 10.1 %all-to-all-start.3 = ((bf16[8,2,1632]{2,1,0:T(2,128)(2,1)}), bf16[8,2,1632]{2,1,0:T(2,128)(2,1)S(1)}, u32[]{:S(2)}, u32[]{:S(2)}) async-start(bf16[8,2,1632]{2,1,0:T(2,128)(2,1)} %reshape.1103), calls=%async_computation.3 | async-start | bytes 106496 | tf_op jit(solution)/shard_map/all_to_all | solution.py:60
  27.8 6.2 %copy-start.14 = (f32[64]{0:T(128)S(1)}, f32[64]{0:T(128)}, u32[]{:S(2)}) copy-start(f32[64]{0:T(128)} %param.31) | copy-start | bytes 772
  27.8 6.2 %copy-start.5 = (f32[4096]{0:T(1024)S(1)}, f32[4096]{0:T(1024)}, u32[]{:S(2)}) copy-start(f32[4096]{0:T(1024)} %param.27) | copy-start | bytes 49156
  27.8 6.3 %copy-start.12 = (f32[64]{0:T(128)S(1)}, f32[64]{0:T(128)}, u32[]{:S(2)}) copy-start(f32[64]{0:T(128)} %param.32) | copy-start | bytes 772
  27.8 6.5 %copy-start.7 = (bf16[2,4,2,128]{3,2,1,0:T(2,128)(2,1)S(1)}, bf16[2,4,2,128]{3,2,1,0:T(2,128)(2,1)}, u32[]{:S(2)}) copy-start(bf16[2,4,2,128]{3,2,1,0:T(2,128)(2,1)} %param.23) | copy-start | bytes 12292
  27.8 6.5 %copy-start.10 = (f32[2,4,64]{2,1,0:T(4,128)S(1)}, f32[2,4,64]{2,1,0:T(4,128)}, u32[]{:S(2)}) copy-start(f32[2,4,64]{2,1,0:T(4,128)} %param.25) | copy-start | bytes 6148
  27.8 6.5 %copy-start.13 = (f32[64]{0:T(128)S(1)}, f32[64]{0:T(128)}, u32[]{:S(2)}) copy-start(f32[64]{0:T(128)} %param.30) | copy-start | bytes 772
  27.8 6.5 %copy-start.3 = (bf16[2,4,4096]{2,1,0:T(4,128)(2,1)S(1)}, bf16[2,4,4096]{2,1,0:T(4,128)(2,1)}, u32[]{:S(2)}) copy-start(bf16[2,4,4096]{2,1,0:T(4,128)(2,1)} %param.22) | copy-start | bytes 196612
  27.8 6.6 %copy-start.4 = (bf16[2,4,4096]{2,1,0:T(4,128)(2,1)S(1)}, bf16[2,4,4096]{2,1,0:T(4,128)(2,1)}, u32[]{:S(2)}) copy-start(bf16[2,4,4096]{2,1,0:T(4,128)(2,1)} %param.24) | copy-start | bytes 196612
  29.8 50.7 %all-to-all-start = ((f32[2,8,32768]{2,0,1:T(2,128)}), f32[2,8,32768]{2,0,1:T(2,128)S(1)}, u32[]{:S(2)}, u32[]{:S(2)}) async-start(f32[2,8,32768]{2,0,1:T(2,128)} %copy.104), calls=%async_computation | async-start | bytes 4194304 | tf_op jit(solution)/shard_map/all_to_all | solution.py:46
  80.5 1.3 copy-start.2
  92.3 4.1 %copy-start.6 = (f32[4,4096]{1,0:T(4,128)S(1)}, f32[4,4096]{1,0:T(4,128)}, u32[]{:S(2)}) copy-start(f32[4,4096]{1,0:T(4,128)} %param.26) | copy-start | bytes 196612
  92.3 6.0 %copy-start.9 = (f32[4,2,128]{2,1,0:T(2,128)S(1)}, f32[4,2,128]{2,1,0:T(2,128)}, u32[]{:S(2)}) copy-start(f32[4,2,128]{2,1,0:T(2,128)} %param.28) | copy-start | bytes 12292
  92.3 6.7 %copy-start.11 = (f32[2,128]{1,0:T(2,128)S(1)}, f32[2,128]{1,0:T(2,128)}, u32[]{:S(2)}) copy-start(f32[2,128]{1,0:T(2,128)} %param.29) | copy-start | bytes 3076
  92.3 52.1 %all-to-all-start.1 = ((f32[16,1,32768]{2,1,0:T(1,128)}), f32[16,1,32768]{2,1,0:T(1,128)S(1)}, u32[]{:S(2)}, u32[]{:S(2)}) async-start(f32[16,1,32768]{2,1,0:T(1,128)} %copy.105), calls=%async_computation.1 | async-start | bytes 4194304 | tf_op jit(solution)/shard_map/all_to_all | solution.py:59
  144.4 1.3 copy-start.1
  165.7 4.5 %copy-start.8 = (f32[4096]{0:T(1024)S(1)}, f32[4096]{0:T(1024)}, u32[]{:S(2)}) copy-start(f32[4096]{0:T(1024)} %param.33) | copy-start | bytes 49156
where the time goes:
time: 196 us; the launch traced here: 195 us
  waiting for transfers between devices  96.6 us (49%)
  local copies, waits for them, and re-layouts  48.9 us (25%)
  other arithmetic  27.6 us (14%)
  starting transfers between devices  18.6 us (9%)
  blocking collectives  2.46 us (1%)
    all_to_all x1, waiting for transfers between devices, on_device(): lax.all_to_all(ssm_state.reshape(slots, owners, -1), 'req', split_axis=1,...  45.1 us
    all_to_all x1, waiting for transfers between devices, on_device(): lax.all_to_all(picked_state, 'req', split_axis=0, concat_axis=1, tiled=True)  45 us
    mul x4, local copies, waits for them, and re-layouts, on_device(): (delta[:, :, None] * heads_x)[..., None] * b_head[:, :, None, :]  17.8 us
    reduce_sum x1, other arithmetic, on_device(): jnp.sum(status * c_head[:, :, None, :], axis=-1)  13.2 us
    all_to_all x1, starting transfers between devices, on_device(): lax.all_to_all(conv_flat.reshape(slots, owners, -1), 'req', split_axis=1,...  7.28 us
    mul x1, other arithmetic, on_device(): new_ssm = status.reshape(places, heads_loc, columns) * mask[:, None, None]  6.13 us
    unnamed x34, local copies, waits for them, and re-layouts  4.76 us
    reshape x2, local copies, waits for them, and re-layouts, on_device(): ssm_state.reshape(slots, owners, -1)  4.69 us
  transfers between devices with their start and end apart: 4, of which 4 were waited for; matrix products, arithmetic and copies ran while one was open for 6% of the time, Pallas kernels for 0%

commit v1 on v0

v1 whole, which is shorter than its diff:
```python
import jax
import jax.numpy as jnp
from jax import lax
from jax.experimental import pallas as pl
from jax.experimental.pallas import tpu as pltpu
from jax.sharding import PartitionSpec as P

H = 128
P_SIZE = 64
STEPS = 4


def ssm_kernel(mask_ref, s_ref, u_ref, dec_ref, b_ref, c_ref, out_ref, y_ref):
    k = pl.program_id(0)
    rows, cols = s_ref.shape[1], s_ref.shape[2]
    seg = u_ref.shape[3]
    lane_seg = lax.broadcasted_iota(jnp.int32, (seg, cols), 1) // (cols // seg)
    expand = (lane_seg == lax.broadcasted_iota(jnp.int32, (seg, cols), 0)).astype(jnp.float32)
    state = s_ref[0]
    for t in range(STEPS):
        upd = jnp.dot(
            u_ref[0, t], expand, precision=lax.Precision.HIGHEST,
            preferred_element_type=jnp.float32,
        )
        state = dec_ref[0, t] * state + upd * b_ref[0, 0, t:t + 1, :]
        prod = state * c_ref[0, 0, t:t + 1, :]
        y_ref[0, t] = lax.dot_general(
            prod, expand, (((1,), (1,)), ((), ())), precision=lax.Precision.HIGHEST,
            preferred_element_type=jnp.float32,
        )
    out_ref[0] = state * mask_ref[k]


def ssm_steps(mask, state, u, dec, bt, ct):
    places, heads, cols = state.shape
    groups = bt.shape[1]
    per = heads // groups
    steps = u.shape[1]
    seg = u.shape[3]
    return pl.pallas_call(
        ssm_kernel,
        grid=(places, groups),
        in_specs=[
            pl.BlockSpec(memory_space=pltpu.SMEM),
            pl.BlockSpec((1, per, cols), lambda k, g: (k, g, 0)),
            pl.BlockSpec((1, steps, per, seg), lambda k, g: (k, 0, g, 0)),
            pl.BlockSpec((1, steps, per, 1), lambda k, g: (k, 0, g, 0)),
            pl.BlockSpec((1, 1, steps, cols), lambda k, g: (k, g, 0, 0)),
            pl.BlockSpec((1, 1, steps, cols), lambda k, g: (k, g, 0, 0)),
        ],
        out_specs=[
            pl.BlockSpec((1, per, cols), lambda k, g: (k, g, 0)),
            pl.BlockSpec((1, steps, per, seg), lambda k, g: (k, 0, g, 0)),
        ],
        out_shape=[
            jax.ShapeDtypeStruct(state.shape, jnp.float32),
            jax.ShapeDtypeStruct(u.shape, jnp.float32),
        ],
    )(mask, state, u, dec, bt, ct)


def migrate(counts, move_plan, ssm_state, conv_flat):
    owners = lax.axis_size("req")
    slots = ssm_state.shape[0]
    places = slots
    reqs = move_plan.shape[0]
    ids = jnp.arange(reqs, dtype=jnp.int32)
    home = ids // slots
    live = ids % slots < jnp.take(counts, home)
    zero_conv = jnp.zeros((), jnp.bfloat16)
    spread_state = lax.all_to_all(
        ssm_state.reshape(slots, owners, -1), "req", split_axis=1, concat_axis=0, tiled=True
    )
    spread_conv = lax.all_to_all(
        conv_flat.reshape(slots, owners, -1), "req", split_axis=1, concat_axis=0, tiled=True
    )
    targets = jnp.arange(owners * places, dtype=jnp.int32)
    match = live[None, :] & (move_plan[None, :] == targets[:, None])
    source = jnp.sum(jnp.where(match, ids[None, :], 0), axis=1)
    hit = jnp.any(match, axis=1)
    keep = hit.astype(jnp.float32)
    picked_state = jnp.take(spread_state, source, axis=0) * keep[:, None, None]
    picked_conv = jnp.where(hit[:, None, None], jnp.take(spread_conv, source, axis=0), zero_conv)
    arrived_state = lax.all_to_all(picked_state, "req", split_axis=0, concat_axis=1, tiled=True)
    arrived_conv = lax.all_to_all(picked_conv, "req", split_axis=0, concat_axis=1, tiled=True)
    owner = lax.axis_index("req")
    mask = lax.dynamic_slice_in_dim(keep, owner * places, places)
    return arrived_state.reshape(ssm_state.shape), arrived_conv.reshape(conv_flat.shape), mask


def on_device(
    counts,
    move_plan,
    ssm_state,
    conv_x_state,
    conv_bc_state,
    x_in,
    bc_in,
    z_in,
    dt_in,
    conv_w_x,
    conv_b_x,
    conv_w_bc,
    conv_b_bc,
    dt_bias,
    a_log,
    d_skip,
    norm_w,
):
    slots, heads_loc, columns = ssm_state.shape
    places, steps, channels = x_in.shape
    groups_loc = conv_bc_state.shape[2]
    pair = conv_bc_state.shape[3]
    state_size = pair // 2
    head_dim = channels // heads_loc
    conv_flat = jnp.concatenate(
        [conv_x_state.reshape(slots, -1), conv_bc_state.reshape(slots, -1)], 1
    )
    state, conv, mask = migrate(counts, move_plan, ssm_state, conv_flat)
    conv_x = conv[:, : 3 * channels].reshape(places, 3, channels)
    conv_bc = conv[:, 3 * channels :].reshape(places, 3, groups_loc, pair)
    per_group = heads_loc // groups_loc

    seq_x = jnp.concatenate([conv_x, x_in], 1)
    seq_bc = jnp.concatenate([conv_bc, bc_in], 1)
    wx = seq_x.astype(jnp.float32)
    wbc = seq_bc.astype(jnp.float32)
    xconv = conv_b_x + sum(wx[:, k:k + steps] * conv_w_x[k] for k in range(4))
    xconv = jax.nn.silu(xconv)
    bconv = conv_b_bc + sum(wbc[:, k:k + steps] * conv_w_bc[k] for k in range(4))
    bconv = jax.nn.silu(bconv)
    delta = jax.nn.softplus(dt_in + dt_bias)
    decay = jnp.exp(-delta * jnp.exp(a_log))
    heads_x = xconv.reshape(places, steps, heads_loc, head_dim)
    u = delta[..., None] * heads_x
    dec = decay[..., None]
    reps = columns // state_size
    bt = jnp.tile(bconv[..., :state_size], (1, 1, 1, reps)).transpose(0, 2, 1, 3)
    ct = jnp.tile(bconv[..., state_size:], (1, 1, 1, reps)).transpose(0, 2, 1, 3)
    new_state, yk = ssm_steps(mask, state, u, dec, bt, ct)
    mixed = yk + d_skip[None, None, :, None] * heads_x
    gated = mixed.reshape(places, steps, channels) * jax.nn.silu(z_in.astype(jnp.float32))
    total = lax.psum(jnp.sum(gated * gated, axis=-1), "tp")
    scaling = 1.0 / (H * P_SIZE)
    normed = gated * lax.rsqrt(total * scaling + 1e-05)[..., None] * norm_w
    y_out = (normed * mask[:, None, None]).astype(jnp.bfloat16)
    filled = mask > 0.5
    new_conv_x = jnp.where(filled[:, None, None], seq_x[:, steps:], jnp.zeros((), jnp.bfloat16))
    new_conv_bc = jnp.where(
        filled[:, None, None, None], seq_bc[:, steps:], jnp.zeros((), jnp.bfloat16)
    )
    return (y_out, new_state, new_conv_x, new_conv_bc)


def solution(mesh):
    in_specs = (
        P("parts"),
        P("parts"),
        P(("parts", "req"), "tp", None),
        P(("parts", "req"), None, "tp"),
        P(("parts", "req"), None, "tp", None),
        P(("parts", "req"), None, "tp"),
        P(("parts", "req"), None, "tp", None),
        P(("parts", "req"), None, "tp"),
        P(("parts", "req"), None, "tp"),
        P(None, "tp"),
        P("tp"),
        P(None, "tp", None),
        P("tp", None),
        P("tp"),
        P("tp"),
        P("tp"),
        P("tp"),
    )
    out_specs = (
        P(("parts", "req"), None, "tp"),
        P(("parts", "req"), "tp", None),
        P(("parts", "req"), None, "tp"),
        P(("parts", "req"), None, "tp", None),
    )
    return jax.shard_map(
        on_device, mesh=mesh, in_specs=in_specs, out_specs=out_specs, check_vma=False
    )
```

time: 196 us -> 165 us (0.84)
  local copies, waits for them, and re-layouts: 48.9 us -> 26.3 us
  other arithmetic: 27.6 us -> 9.11 us
  Pallas kernels: 0 us -> 17.9 us
  waiting for transfers between devices: 96.6 us -> 86.9 us
  starting transfers between devices: 18.6 us -> 21.1 us
    mul x7 -> x2, local copies, waits for them, and re-layouts: 21.4 us -> 3.48 us  [the longest x1 3.48 us: migrate(): picked_state = jnp.take(spread_state, source, axis=0) * keep[:, None, None]]
    pallas_call x0 -> x1, Pallas kernels: none -> 17.9 us  [ssm_steps(): pl.pallas_call(ssm_kernel, grid=(places, groups), in_specs=[pl.BlockSpec(...]
    reduce_sum x4 -> x1, other arithmetic: 14.7 us -> 0.12 us  [migrate(): source = jnp.sum(jnp.where(match, ids[None, :], 0), axis=1)]
    all_to_all x4, waiting for transfers between devices: 96.6 us -> 86.9 us  [the longest x1 43 us: migrate(): lax.all_to_all(picked_state, 'req', split_axis=0, concat_axis=1, tiled=True)]
    mul x5 -> x4, other arithmetic: 8.43 us -> 2.84 us  [the longest x1 1.8 us: migrate(): picked_state = jnp.take(spread_state, source, axis=0) * keep[:, None, None]]
    unnamed x34, local copies, waits for them, and re-layouts: 4.76 us -> 0.77 us
    reshape x5 -> x8, local copies, waits for them, and re-layouts: 5.68 us -> 8.74 us  [the longest x2 4.69 us: migrate(): ssm_state.reshape(slots, owners, -1)]
    another operation x2 -> x4, local copies, waits for them, and re-layouts: 4.6 us -> 1.96 us  [the longest x2 0.98 us: on_device(): jnp.tile(bconv[..., state_size:], (1, 1, 1, reps)).transpose(0, 2, 1, 3)]
  transfers between devices with their start and end apart: 4 -> 4, of which waited for: 4 -> 3; matrix products, arithmetic and copies ran while one was open for 6% -> 15% of each run, Pallas kernels for 0% -> 0%
where the time goes in v1:
time: 165 us
  waiting for transfers between devices  86.9 us (53%)
  local copies, waits for them, and re-layouts  26.3 us (16%)
  starting transfers between devices  21.1 us (13%)
  Pallas kernels  17.9 us (11%)
  other arithmetic  9.11 us (6%)
  blocking collectives  2.45 us (1%)
    all_to_all x1, waiting for transfers between devices, migrate(): lax.all_to_all(picked_state, 'req', split_axis=0, concat_axis=1, tiled=True)  43 us
    all_to_all x1, waiting for transfers between devices, migrate(): lax.all_to_all(ssm_state.reshape(slots, owners, -1), 'req', split_axis=1,...  41.9 us
    pallas_call x1, Pallas kernels, ssm_steps(): pl.pallas_call(ssm_kernel, grid=(places, groups), in_specs=[pl.BlockSpec(...  17.9 us
    all_to_all x1, starting transfers between devices, migrate(): lax.all_to_all(conv_flat.reshape(slots, owners, -1), 'req', split_axis=1,...  7.28 us
    all_to_all x1, starting transfers between devices, migrate(): lax.all_to_all(picked_state, 'req', split_axis=0, concat_axis=1, tiled=True)  6.12 us
    reshape x2, local copies, waits for them, and re-layouts, migrate(): ssm_state.reshape(slots, owners, -1)  4.69 us
    all_to_all x1, starting transfers between devices, migrate(): lax.all_to_all(ssm_state.reshape(slots, owners, -1), 'req', split_axis=1,...  4.07 us
    all_to_all x1, starting transfers between devices, migrate(): lax.all_to_all(picked_conv, 'req', split_axis=0, concat_axis=1, tiled=True)  3.64 us
  transfers between devices with their start and end apart: 4, of which 3 were waited for; matrix products, arithmetic and copies ran while one was open for 15% of the time, Pallas kernels for 0%

profile of v1, /device:TPU:0, one launch (start us, length us, event | category | flops | bytes accessed | tf_op | source)
XLA Modules:
  0.0 164.8 jit_solution(4069765433226081546)
XLA Ops:
  0.6 0.7 reshape.267
  1.4 0.8 pad_maximum_fusion
  2.4 0.7 copy.65
  3.0 7.3 %all-to-all-start.2 = ((bf16[2,8,1632]{2,0,1:T(2,128)(2,1)}), bf16[2,8,1632]{2,0,1:T(2,128)(2,1)S(1)}, u32[]{:S(2)}, u32[]{:S(2)}) async-start(bf16[2,8,1632]{2,0,1:T(2,128)(2,1)} %copy.65), calls=%async_computation.2 | async-start | bytes 106496 | tf_op jit(solution)/shard_map/all_to_all | solution.py:74
  10.3 1.7 %reshape.264 = f32[2,8,32768]{2,1,0:T(8,128)S(1)} reshape(f32[2,64,4096]{2,1,0:T(8,128)} %param.19) | data formatting | bytes 4194304 | tf_op jit(solution)/shard_map/reshape | solution.py:72
  12.1 2.9 %copy.62 = f32[2,8,32768]{2,0,1:T(2,128)} copy(f32[2,8,32768]{2,1,0:T(8,128)S(1)} %reshape.264) | data formatting | bytes 4194304 | tf_op jit(solution)/shard_map/reshape | solution.py:72
  15.1 2.1 %all-to-all-done.2 = bf16[2,8,1632]{2,0,1:T(2,128)(2,1)S(1)} async-done(((bf16[2,8,1632]{2,0,1:T(2,128)(2,1)}), bf16[2,8,1632]{2,0,1:T(2,128)(2,1)S(1)}, u32[]{:S(2)}, u32[]{:S(2)}) %all-to-all-start.2) | async-done | bytes 52256 | tf_op jit(solution)/shard_map/all_to_all | solution.py:74
  17.1 4.1 %all-to-all-start = ((f32[2,8,32768]{2,0,1:T(2,128)}), f32[2,8,32768]{2,0,1:T(2,128)S(1)}, u32[]{:S(2)}, u32[]{:S(2)}) async-start(f32[2,8,32768]{2,0,1:T(2,128)} %copy.62), calls=%async_computation | async-start | bytes 4194304 | tf_op jit(solution)/shard_map/all_to_all | solution.py:71
  21.3 0.7 gather_fusion
  22.1 0.9 copy.70.dec_ref
  23.8 0.7 broadcast_select_fusion.1
  24.5 0.6 gather_fusion.2
  25.7 0.7 reduce.1
  26.4 0.6 reshape.305
  27.0 41.9 %all-to-all-done = f32[2,8,32768]{2,0,1:T(2,128)S(1)} async-done(((f32[2,8,32768]{2,0,1:T(2,128)}), f32[2,8,32768]{2,0,1:T(2,128)S(1)}, u32[]{:S(2)}, u32[]{:S(2)}) %all-to-all-start) | async-done | bytes 2097184 | tf_op jit(solution)/shard_map/all_to_all | solution.py:71
  68.9 3.6 %all-to-all-start.3 = ((bf16[8,2,1632]{2,1,0:T(2,128)(2,1)}), bf16[8,2,1632]{2,1,0:T(2,128)(2,1)S(1)}, u32[]{:S(2)}, u32[]{:S(2)}) async-start(bf16[8,2,1632]{2,1,0:T(2,128)(2,1)} %reshape.305), calls=%async_computation.3 | async-start | bytes 106496 | tf_op jit(solution)/shard_map/all_to_all | solution.py:85
  72.5 2.7 %reshape.282 = f32[16,32768]{1,0:T(8,128)S(1)} reshape(f32[8,2,1,32768]{3,1,0,2:T(2,128)} %bitcast.64) | data formatting | bytes 4194304 | tf_op jit(solution)/shard_map/all_to_all | solution.py:71
  75.2 2.4 %gather_fusion.1 = f32[16,32768]{1,0:T(8,128)} fusion(f32[16,32768]{1,0:T(8,128)S(1)} %reshape.282, s32[1024]{0:T(1024)S(1)} %pad_clamp_fusion), kind=kCustom, calls=%fused_computation.1 | custom fusion | bytes 4194368 | tf_op jit(solution)/shard_map/jit(_take)/gather | solution.py:82
  77.6 1.8 %fusion = f32[16,1,32768]{2,0,1:T(8,128)S(1)} fusion(f32[16,32768]{1,0:T(8,128)} %gather_fusion.1, f32[16]{0:T(128)S(1)} %convert_element_type.19, pred[16]{0:T(512)(128)(4,1)S(1)} %compare_and_fusion), kind=kLoop, calls=%fused_computation.4 | loop fusion | flops 1048576 | bytes 4194384 | tf_op jit(solution)/shard_map/mul | solution.py:82
  79.4 3.5 %copy.63 = f32[16,1,32768]{2,1,0:T(1,128)} copy(f32[16,1,32768]{2,0,1:T(8,128)S(1)} %fusion) | data formatting | bytes 4194304 | tf_op jit(solution)/shard_map/mul | solution.py:82
  82.9 6.1 %all-to-all-start.1 = ((f32[16,1,32768]{2,1,0:T(1,128)}), f32[16,1,32768]{2,1,0:T(1,128)S(1)}, u32[]{:S(2)}, u32[]{:S(2)}) async-start(f32[16,1,32768]{2,1,0:T(1,128)} %copy.63), calls=%async_computation.1 | async-start | bytes 4194304 | tf_op jit(solution)/shard_map/all_to_all | solution.py:84
  89.1 0.7 broadcast_select_fusion
  91.2 0.9 tile.9
  92.2 0.9 tile.21
  93.1 0.8 broadcast_multiply_fusion.u_ref
  94.0 43.0 %all-to-all-done.1 = f32[16,1,32768]{2,1,0:T(1,128)S(1)} async-done(((f32[16,1,32768]{2,1,0:T(1,128)}), f32[16,1,32768]{2,1,0:T(1,128)S(1)}, u32[]{:S(2)}, u32[]{:S(2)}) %all-to-all-start.1) | async-done | bytes 2097184 | tf_op jit(solution)/shard_map/all_to_all | solution.py:84
  136.9 2.5 %copy.76 = f32[8,2,1,32768]{3,0,1,2:T(8,128)} copy(f32[8,2,1,32768]{3,2,1,0:T(1,128)S(1)} %bitcast.65) | data formatting | bytes 4194304 | tf_op jit(solution)/shard_map/all_to_all | solution.py:84
  139.5 2.7 %reshape.265.s_ref = f32[2,64,4096]{2,1,0:T(8,128)} reshape(f32[2,8,1,32768]{3,1,0,2:T(8,128)} %bitcast.66) | data formatting | bytes 4194304 | tf_op jit(solution)/shard_map/reshape | solution.py:88
  142.2 17.9 %shard_map.192 = (f32[2,64,4096]{2,1,0:T(8,128)}, f32[2,4,64,64]{3,2,1,0:T(8,128)}) custom-call(f32[2]{0:T(128)} %get-tuple-element.9.mask_ref, f32[2,64,4096]{2,1,0:T(8,128)} %reshape.265.s_ref, f32[2,4,64,64]{3,2,1,0:T(8,128)} %broadcast_multiply_fusion.u_ref, f32[2,4,64,1]{3,2,1,0:T(8,128)} %copy.70.dec_ref, f32[2,2,4,4096]{3,2,1,0:T(4,128)} %bitcast.67, ...), custom_call_target="tpu_custom_call" | custom-call | tf_op jit(solution)/shard_map/pallas_call | solution.py:40
  160.2 1.1 multiply_add_fusion
  161.6 2.4 %psum.7 = f32[2,4]{1,0:T(2,128)S(1)} all-reduce(f32[2,4]{1,0:T(2,128)S(1)} %get-tuple-element.10), channel_id=1, replica_groups=mesh['parts'=2,'req'=8,'tp'=2] {'tp'}, use_global_device_ids=true, to_apply=%region_3.4 | all-reduce | flops 8 | bytes 64 | tf_op jit(solution)/shard_map/psum | solution.py:143
  164.0 0.7 multiply_convert_fusion
  (74 shorter events, 3.5 us)
Async XLA Ops:
  0.6 20.6 %copy-start = (s32[8]{0:T(128)S(1)}, s32[8]{0:T(128)}, u32[]{:S(2)}) copy-start(s32[8]{0:T(128)} %param.17) | copy-start | bytes 100
  3.0 14.1 %all-to-all-start.2 = ((bf16[2,8,1632]{2,0,1:T(2,128)(2,1)}), bf16[2,8,1632]{2,0,1:T(2,128)(2,1)S(1)}, u32[]{:S(2)}, u32[]{:S(2)}) async-start(bf16[2,8,1632]{2,0,1:T(2,128)(2,1)} %copy.65), calls=%async_computation.2 | async-start | bytes 106496 | tf_op jit(solution)/shard_map/all_to_all | solution.py:74
  15.0 6.2 %copy-start.14 = (f32[64]{0:T(128)S(1)}, f32[64]{0:T(128)}, u32[]{:S(2)}) copy-start(f32[64]{0:T(128)} %param.31) | copy-start | bytes 772
  15.0 6.9 %copy-start.15 = (s32[16]{0:T(128)S(1)}, s32[16]{0:T(128)}, u32[]{:S(2)}) copy-start(s32[16]{0:T(128)} %param.18) | copy-start | bytes 196
  15.0 7.1 %copy-start.9 = (f32[2,4,64]{2,1,0:T(4,128)S(1)}, f32[2,4,64]{2,1,0:T(4,128)}, u32[]{:S(2)}) copy-start(f32[2,4,64]{2,1,0:T(4,128)} %param.25) | copy-start | bytes 6148
  15.0 7.1 %copy-start.12 = (f32[64]{0:T(128)S(1)}, f32[64]{0:T(128)}, u32[]{:S(2)}) copy-start(f32[64]{0:T(128)} %param.30) | copy-start | bytes 772
  15.0 8.0 %copy-start.2 = (bf16[2,4,4096]{2,1,0:T(4,128)(2,1)S(1)}, bf16[2,4,4096]{2,1,0:T(4,128)(2,1)}, u32[]{:S(2)}) copy-start(bf16[2,4,4096]{2,1,0:T(4,128)(2,1)} %param.22) | copy-start | bytes 196612
  15.0 8.7 %copy-start.10 = (f32[4,2,128]{2,1,0:T(2,128)S(1)}, f32[4,2,128]{2,1,0:T(2,128)}, u32[]{:S(2)}) copy-start(f32[4,2,128]{2,1,0:T(2,128)} %param.28) | copy-start | bytes 12292
  15.0 8.8 %copy-start.7 = (bf16[2,4,2,128]{3,2,1,0:T(2,128)(2,1)S(1)}, bf16[2,4,2,128]{3,2,1,0:T(2,128)(2,1)}, u32[]{:S(2)}) copy-start(bf16[2,4,2,128]{3,2,1,0:T(2,128)(2,1)} %param.23) | copy-start | bytes 12292
  17.1 51.7 %all-to-all-start = ((f32[2,8,32768]{2,0,1:T(2,128)}), f32[2,8,32768]{2,0,1:T(2,128)S(1)}, u32[]{:S(2)}, u32[]{:S(2)}) async-start(f32[2,8,32768]{2,0,1:T(2,128)} %copy.62), calls=%async_computation | async-start | bytes 4194304 | tf_op jit(solution)/shard_map/all_to_all | solution.py:71
  68.9 3.6 %copy-start.1 = (f32[2,8,32768]{2,0,1:T(2,128)}, f32[2,8,32768]{2,0,1:T(2,128)S(1)}, u32[]{:S(2)}) copy-start(f32[2,8,32768]{2,0,1:T(2,128)S(1)} %all-to-all-done) | copy-start | bytes 6291460
  68.9 14.1 %all-to-all-start.3 = ((bf16[8,2,1632]{2,1,0:T(2,128)(2,1)}), bf16[8,2,1632]{2,1,0:T(2,128)(2,1)S(1)}, u32[]{:S(2)}, u32[]{:S(2)}) async-start(bf16[8,2,1632]{2,1,0:T(2,128)(2,1)} %reshape.305), calls=%async_computation.3 | async-start | bytes 106496 | tf_op jit(solution)/shard_map/all_to_all | solution.py:85
  82.9 6.9 %copy-start.4 = (f32[4,4096]{1,0:T(4,128)S(1)}, f32[4,4096]{1,0:T(4,128)}, u32[]{:S(2)}) copy-start(f32[4,4096]{1,0:T(4,128)} %param.26) | copy-start | bytes 196612
  82.9 7.7 %copy-start.5 = (f32[4096]{0:T(1024)S(1)}, f32[4096]{0:T(1024)}, u32[]{:S(2)}) copy-start(f32[4096]{0:T(1024)} %param.27) | copy-start | bytes 49156
  82.9 54.0 %all-to-all-start.1 = ((f32[16,1,32768]{2,1,0:T(1,128)}), f32[16,1,32768]{2,1,0:T(1,128)S(1)}, u32[]{:S(2)}, u32[]{:S(2)}) async-start(f32[16,1,32768]{2,1,0:T(1,128)} %copy.63), calls=%async_computation.1 | async-start | bytes 4194304 | tf_op jit(solution)/shard_map/all_to_all | solution.py:84
  89.1 2.0 %copy-start.11 = (f32[2,128]{1,0:T(2,128)S(1)}, f32[2,128]{1,0:T(2,128)}, u32[]{:S(2)}) copy-start(f32[2,128]{1,0:T(2,128)} %param.29) | copy-start | bytes 3076
  142.2 18.0 %copy-start.13 = (f32[64]{0:T(128)S(1)}, f32[64]{0:T(128)}, u32[]{:S(2)}) copy-start(f32[64]{0:T(128)} %param.32) | copy-start | bytes 772
  142.2 19.2 %copy-start.3 = (bf16[2,4,4096]{2,1,0:T(4,128)(2,1)S(1)}, bf16[2,4,4096]{2,1,0:T(4,128)(2,1)}, u32[]{:S(2)}) copy-start(bf16[2,4,4096]{2,1,0:T(4,128)(2,1)} %param.24) | copy-start | bytes 196612
  142.2 21.8 %copy-start.6 = (f32[4096]{0:T(1024)S(1)}, f32[4096]{0:T(1024)}, u32[]{:S(2)}) copy-start(f32[4096]{0:T(1024)} %param.33) | copy-start | bytes 49156
  142.2 21.8 %copy-start.8 = (f32[2]{0:T(128)S(1)}, f32[2]{0:T(128)}, u32[]{:S(2)}) copy-start(f32[2]{0:T(128)} %get-tuple-element.9.mask_ref) | copy-start | bytes 28

commit v2 on v1

--- a/solution.py
+++ b/solution.py
@@ -10,13 +10,14 @@
 STEPS = 4
 
 
-def ssm_kernel(mask_ref, s_ref, u_ref, dec_ref, b_ref, c_ref, out_ref, y_ref):
+def ssm_kernel(sel_ref, s_ref, r_ref, u_ref, dec_ref, b_ref, c_ref, out_ref, y_ref):
     k = pl.program_id(0)
+    places = pl.num_programs(0)
     rows, cols = s_ref.shape[1], s_ref.shape[2]
     seg = u_ref.shape[3]
     lane_seg = lax.broadcasted_iota(jnp.int32, (seg, cols), 1) // (cols // seg)
     expand = (lane_seg == lax.broadcasted_iota(jnp.int32, (seg, cols), 0)).astype(jnp.float32)
-    state = s_ref[0]
+    state = jnp.where(sel_ref[places + k] == 1, r_ref[0], s_ref[0])
     for t in range(STEPS):
         upd = jnp.dot(
             u_ref[0, t], expand, precision=lax.Precision.HIGHEST,
@@ -28,64 +29,83 @@
             prod, expand, (((1,), (1,)), ((), ())), precision=lax.Precision.HIGHEST,
             preferred_element_type=jnp.float32,
         )
-    out_ref[0] = state * mask_ref[k]
-
-
-def ssm_steps(mask, state, u, dec, bt, ct):
+    keep = (sel_ref[2 * places + k] == 1).astype(jnp.float32)
+    out_ref[0] = state * keep
+
+
+def ssm_steps(sel, state, recv, u, dec, bt, ct):
     places, heads, cols = state.shape
     groups = bt.shape[1]
     per = heads // groups
     steps = u.shape[1]
     seg = u.shape[3]
+    grid_spec = pltpu.PrefetchScalarGridSpec(
+        num_scalar_prefetch=1,
+        grid=(places, groups),
+        in_specs=[
+            pl.BlockSpec((1, per, cols), lambda k, g, s: (s[k], g, 0)),
+            pl.BlockSpec((1, per, cols), lambda k, g, s: (0, g, 0)),
+            pl.BlockSpec((1, steps, per, seg), lambda k, g, s: (k, 0, g, 0)),
+            pl.BlockSpec((1, steps, per, 1), lambda k, g, s: (k, 0, g, 0)),
+            pl.BlockSpec((1, 1, steps, cols), lambda k, g, s: (k, g, 0, 0)),
+            pl.BlockSpec((1, 1, steps, cols), lambda k, g, s: (k, g, 0, 0)),
+        ],
+        out_specs=[
+            pl.BlockSpec((1, per, cols), lambda k, g, s: (k, g, 0)),
+            pl.BlockSpec((1, steps, per, seg), lambda k, g, s: (k, 0, g, 0)),
+        ],
+    )
     return pl.pallas_call(
         ssm_kernel,
-        grid=(places, groups),
-        in_specs=[
-            pl.BlockSpec(memory_space=pltpu.SMEM),
-            pl.BlockSpec((1, per, cols), lambda k, g: (k, g, 0)),
-            pl.BlockSpec((1, steps, per, seg), lambda k, g: (k, 0, g, 0)),
-            pl.BlockSpec((1, steps, per, 1), lambda k, g: (k, 0, g, 0)),
-            pl.BlockSpec((1, 1, steps, cols), lambda k, g: (k, g, 0, 0)),
-            pl.BlockSpec((1, 1, steps, cols), lambda k, g: (k, g, 0, 0)),
-        ],
-        out_specs=[
-            pl.BlockSpec((1, per, cols), lambda k, g: (k, g, 0)),
-            pl.BlockSpec((1, steps, per, seg), lambda k, g: (k, 0, g, 0)),
-        ],
+        grid_spec=grid_spec,
         out_shape=[
             jax.ShapeDtypeStruct(state.shape, jnp.float32),
             jax.ShapeDtypeStruct(u.shape, jnp.float32),
         ],
-    )(mask, state, u, dec, bt, ct)
+    )(sel, state, recv, u, dec, bt, ct)
 
 
 def migrate(counts, move_plan, ssm_state, conv_flat):
     owners = lax.axis_size("req")
     slots = ssm_state.shape[0]
-    places = slots
     reqs = move_plan.shape[0]
+    owner = lax.axis_index("req")
     ids = jnp.arange(reqs, dtype=jnp.int32)
     home = ids // slots
     live = ids % slots < jnp.take(counts, home)
-    zero_conv = jnp.zeros((), jnp.bfloat16)
+    dest_owner = move_plan // slots
+    outgoing = live & (home == owner) & (dest_owner != owner)
+    send_j = jnp.sum(jnp.where(outgoing, ids, 0)) % slots
+    owner_ids = jnp.arange(owners, dtype=jnp.int32)
+    incoming = (
+        live[None, :]
+        & (dest_owner[None, :] == owner_ids[:, None])
+        & (home[None, :] != owner_ids[:, None])
+    )
+    src_owner = jnp.sum(jnp.where(incoming, ids[None, :], 0), axis=1) // slots
+    out_state = lax.dynamic_index_in_dim(ssm_state, send_j, 0, keepdims=False)
+    out_conv = lax.dynamic_index_in_dim(conv_flat, send_j, 0, keepdims=False)
     spread_state = lax.all_to_all(
-        ssm_state.reshape(slots, owners, -1), "req", split_axis=1, concat_axis=0, tiled=True
+        out_state.reshape(owners, -1), "req", split_axis=0, concat_axis=0, tiled=True
     )
     spread_conv = lax.all_to_all(
-        conv_flat.reshape(slots, owners, -1), "req", split_axis=1, concat_axis=0, tiled=True
-    )
-    targets = jnp.arange(owners * places, dtype=jnp.int32)
+        out_conv.reshape(owners, -1), "req", split_axis=0, concat_axis=0, tiled=True
+    )
+    picked_state = jnp.take(spread_state, src_owner, axis=0)
+    picked_conv = jnp.take(spread_conv, src_owner, axis=0)
+    rstate = lax.all_to_all(picked_state, "req", split_axis=0, concat_axis=0, tiled=True)
+    rconv = lax.all_to_all(picked_conv, "req", split_axis=0, concat_axis=0, tiled=True)
+    rstate = rstate.reshape((1,) + ssm_state.shape[1:])
+    rconv = rconv.reshape(1, -1)
+    targets = owner * slots + jnp.arange(slots, dtype=jnp.int32)
     match = live[None, :] & (move_plan[None, :] == targets[:, None])
+    hit = jnp.any(match, axis=1)
     source = jnp.sum(jnp.where(match, ids[None, :], 0), axis=1)
-    hit = jnp.any(match, axis=1)
-    keep = hit.astype(jnp.float32)
-    picked_state = jnp.take(spread_state, source, axis=0) * keep[:, None, None]
-    picked_conv = jnp.where(hit[:, None, None], jnp.take(spread_conv, source, axis=0), zero_conv)
-    arrived_state = lax.all_to_all(picked_state, "req", split_axis=0, concat_axis=1, tiled=True)
-    arrived_conv = lax.all_to_all(picked_conv, "req", split_axis=0, concat_axis=1, tiled=True)
-    owner = lax.axis_index("req")
-    mask = lax.dynamic_slice_in_dim(keep, owner * places, places)
-    return arrived_state.reshape(ssm_state.shape), arrived_conv.reshape(conv_flat.shape), mask
+    use_recv = hit & (source // slots != owner)
+    local = jnp.where(hit & ~use_recv, source % slots, 0)
+    sel = jnp.concatenate([local, use_recv.astype(jnp.int32), hit.astype(jnp.int32)])
+    conv = jnp.where(use_recv[:, None], rconv, jnp.take(conv_flat, local, axis=0))
+    return sel, rstate, conv, hit.astype(jnp.float32)
 
 
 def on_device(
@@ -116,7 +136,7 @@
     conv_flat = jnp.concatenate(
         [conv_x_state.reshape(slots, -1), conv_bc_state.reshape(slots, -1)], 1
     )
-    state, conv, mask = migrate(counts, move_plan, ssm_state, conv_flat)
+    sel, recv, conv, mask = migrate(counts, move_plan, ssm_state, conv_flat)
     conv_x = conv[:, : 3 * channels].reshape(places, 3, channels)
     conv_bc = conv[:, 3 * channels :].reshape(places, 3, groups_loc, pair)
     per_group = heads_loc // groups_loc
@@ -137,7 +157,7 @@
     reps = columns // state_size
     bt = jnp.tile(bconv[..., :state_size], (1, 1, 1, reps)).transpose(0, 2, 1, 3)
     ct = jnp.tile(bconv[..., state_size:], (1, 1, 1, reps)).transpose(0, 2, 1, 3)
-    new_state, yk = ssm_steps(mask, state, u, dec, bt, ct)
+    new_state, yk = ssm_steps(sel, ssm_state, recv, u, dec, bt, ct)
     mixed = yk + d_skip[None, None, :, None] * heads_x
     gated = mixed.reshape(places, steps, channels) * jax.nn.silu(z_in.astype(jnp.float32))
     total = lax.psum(jnp.sum(gated * gated, axis=-1), "tp")

time: 165 us -> 127 us (0.77)
  waiting for transfers between devices: 86.9 us -> 49.9 us
  local copies, waits for them, and re-layouts: 26.3 us -> 17.2 us
  other arithmetic: 9.11 us -> 14.7 us
  between operations: 0.95 us -> 2.98 us
    all_to_all x4, waiting for transfers between devices: 86.9 us -> 49.9 us  [the longest x1 24.3 us: migrate(): lax.all_to_all(out_state.reshape(owners, -1), 'req', split_axis=0, concat...]
    reshape x6 -> x1, local copies, waits for them, and re-layouts: 8.42 us -> 1.19 us  [migrate(): rstate = rstate.reshape((1,) + ssm_state.shape[1:])]
    mul x1 -> x0, local copies, waits for them, and re-layouts: 3.48 us -> none  [migrate(): picked_state = jnp.take(spread_state, source, axis=0) * keep[:, None, None]]
    all_to_all x1 -> x3, other arithmetic: 0.31 us -> 3.55 us  [the longest x1 2.61 us: migrate(): lax.all_to_all(picked_state, 'req', split_axis=0, concat_axis=0, tiled=True)]
    all_to_all x5 -> x3, local copies, waits for them, and re-layouts: 5.32 us -> 2.83 us  [the longest x1 2.22 us: migrate(): lax.all_to_all(out_state.reshape(owners, -1), 'req', split_axis=0, concat...]
    unnamed x34 -> x32, local copies, waits for them, and re-layouts: 0.77 us -> 2.85 us
    mul x1 -> x0, other arithmetic: 1.8 us -> none  [migrate(): picked_state = jnp.take(spread_state, source, axis=0) * keep[:, None, None]]
  transfers between devices with their start and end apart: 4 -> 4, of which waited for: 3 -> 4; matrix products, arithmetic and copies ran while one was open for 15% -> 9% of each run, Pallas kernels for 0% -> 0%
where the time goes in v2:
time: 127 us; the launch traced here: 126 us
  waiting for transfers between devices  49.9 us (39%)
  starting transfers between devices  19.8 us (16%)
  Pallas kernels  18.9 us (15%)
  local copies, waits for them, and re-layouts  17.2 us (14%)
  other arithmetic  14.7 us (12%)
  between operations  2.98 us (2%)
  blocking collectives  2.45 us (2%)
    all_to_all x1, waiting for transfers between devices, migrate(): lax.all_to_all(out_state.reshape(owners, -1), 'req', split_axis=0, concat...  24.3 us
    all_to_all x1, waiting for transfers between devices, migrate(): lax.all_to_all(picked_state, 'req', split_axis=0, concat_axis=0, tiled=True)  22.3 us
    pallas_call x1, Pallas kernels, ssm_steps(): pl.pallas_call(ssm_kernel, grid_spec=grid_spec, out_shape=[jax.ShapeDtype...  18.9 us
    all_to_all x1, starting transfers between devices, migrate(): lax.all_to_all(out_conv.reshape(owners, -1), 'req', split_axis=0, concat_...  7.28 us
    all_to_all x1, starting transfers between devices, migrate(): lax.all_to_all(picked_conv, 'req', split_axis=0, concat_axis=0, tiled=True)  5.03 us
    all_to_all x1, starting transfers between devices, migrate(): lax.all_to_all(picked_state, 'req', split_axis=0, concat_axis=0, tiled=True)  3.87 us
    all_to_all x1, starting transfers between devices, migrate(): lax.all_to_all(out_state.reshape(owners, -1), 'req', split_axis=0, concat...  3.65 us
    unnamed x32, local copies, waits for them, and re-layouts  2.85 us
  transfers between devices with their start and end apart: 4, of which 4 were waited for; matrix products, arithmetic and copies ran while one was open for 9% of the time, Pallas kernels for 0%

profile of v2, /device:TPU:0, one launch (start us, length us, event | category | flops | bytes accessed | tf_op | source)
XLA Modules:
  0.0 126.0 jit_solution(7896667002988849402)
XLA Ops:
  2.0 1.3 %fusion.22 = (s32[]{:T(128)}, s32[16]{0:T(128)S(1)}, pred[16]{0:T(512)(128)(4,1)S(1)}, s32[16]{0:T(128)S(1)}) fusion(s32[]{:T(128)S(6)} %axis_index.15, s32[16]{0:T(128)} %param.18, s32[16]{0:T(128)S(1)} %gather_fusion), kind=kLoop, calls=%fused_computation.118 | loop fusion | flops 655 | bytes 280 | tf_op jit(solution)/shard_map/reduce_sum | solution.py:78
  5.2 0.7 reshape.384
  5.9 1.0 maximum_reduce_fusion
  7.5 0.8 reduce.4
  8.3 0.7 reshape.424
  9.0 7.3 %all-to-all-start.2 = ((bf16[8,2,816]{2,1,0:T(2,128)(2,1)}), bf16[8,2,816]{2,1,0:T(2,128)(2,1)S(1)}, u32[]{:S(2)}, u32[]{:S(2)}) async-start(bf16[8,2,816]{2,1,0:T(2,128)(2,1)} %reshape.424), calls=%async_computation.2 | async-start | bytes 57344 | tf_op jit(solution)/shard_map/all_to_all | solution.py:91
  16.5 0.8 fusion.17
  17.3 0.8 fusion.16
  18.2 0.8 pad_maximum_fusion
  19.1 1.3 %constant_dynamic-slice_fusion = f32[1,64,4096]{2,1,0:T(8,128)S(1)} fusion(f32[2,64,4096]{2,1,0:T(8,128)} %s_ref.1, s32[]{:T(128)S(6)} %select_n.249), kind=kLoop, calls=%fused_computation.108 | loop fusion | bytes 2097156 | tf_op jit(solution)/shard_map/jit(dynamic_index_in_dim)/dynamic_slice | solution.py:86
  20.6 0.7 broadcast_select_fusion.2
  22.0 1.0 all-to-all-done.2
  24.4 0.7 reshape.426
  25.1 5.0 %all-to-all-start.3 = ((bf16[8,2,816]{2,1,0:T(2,128)(2,1)}), bf16[8,2,816]{2,1,0:T(2,128)(2,1)S(1)}, u32[]{:S(2)}, u32[]{:S(2)}) async-start(bf16[8,2,816]{2,1,0:T(2,128)(2,1)} %reshape.426), calls=%async_computation.3 | async-start | bytes 57344 | tf_op jit(solution)/shard_map/all_to_all | solution.py:97
  30.7 2.2 %all_to_all.24 = f32[8,1,32768]{2,1,0:T(1,128)} reshape(f32[1,64,4096]{2,1,0:T(8,128)S(1)} %constant_dynamic-slice_fusion) | data formatting | bytes 2097152 | tf_op jit(solution)/shard_map/all_to_all | solution.py:88
  33.0 0.9 copy.51.dec_ref
  34.4 2.4 %all-to-all-done.3 = bf16[8,2,816]{2,1,0:T(2,128)(2,1)S(1)} async-done(((bf16[8,2,816]{2,1,0:T(2,128)(2,1)}), bf16[8,2,816]{2,1,0:T(2,128)(2,1)S(1)}, u32[]{:S(2)}, u32[]{:S(2)}) %all-to-all-start.3) | async-done | bytes 26144 | tf_op jit(solution)/shard_map/all_to_all | solution.py:97
  36.8 3.7 %all-to-all-start = ((f32[8,1,32768]{2,1,0:T(1,128)}), f32[8,1,32768]{2,1,0:T(1,128)S(1)}, u32[]{:S(2)}, u32[]{:S(2)}) async-start(f32[8,1,32768]{2,1,0:T(1,128)} %all_to_all.24), calls=%async_computation | async-start | bytes 2097152 | tf_op jit(solution)/shard_map/all_to_all | solution.py:88
  41.0 24.3 %all-to-all-done = f32[8,1,32768]{2,1,0:T(1,128)S(1)} async-done(((f32[8,1,32768]{2,1,0:T(1,128)}), f32[8,1,32768]{2,1,0:T(1,128)S(1)}, u32[]{:S(2)}, u32[]{:S(2)}) %all-to-all-start) | async-done | bytes 1048608 | tf_op jit(solution)/shard_map/all_to_all | solution.py:88
  65.9 0.9 gather_fusion.1
  67.0 2.0 %copy.45 = f32[8,1,32768]{2,1,0:T(1,128)} copy(f32[8,1,32768]{2,0,1:T(8,128)S(1)} %bitcast_select_fusion) | data formatting | bytes 2097152 | tf_op jit(solution)/shard_map/jit(_take)/select_n | solution.py:94
  69.1 3.9 %all-to-all-start.1 = ((f32[8,1,32768]{2,1,0:T(1,128)}), f32[8,1,32768]{2,1,0:T(1,128)S(1)}, u32[]{:S(2)}, u32[]{:S(2)}) async-start(f32[8,1,32768]{2,1,0:T(1,128)} %copy.45), calls=%async_computation.1 | async-start | bytes 2097152 | tf_op jit(solution)/shard_map/all_to_all | solution.py:96
  73.6 0.9 tile.9
  74.6 0.9 tile.21
  75.5 0.9 broadcast_multiply_fusion.u_ref
  76.4 22.3 %all-to-all-done.1 = f32[8,1,32768]{2,1,0:T(1,128)S(1)} async-done(((f32[8,1,32768]{2,1,0:T(1,128)}), f32[8,1,32768]{2,1,0:T(1,128)S(1)}, u32[]{:S(2)}, u32[]{:S(2)}) %all-to-all-start.1) | async-done | bytes 1048608 | tf_op jit(solution)/shard_map/all_to_all | solution.py:96
  98.7 2.6 %reduce = f32[8,32768]{1,0:T(8,128)S(1)} reduce(f32[8,1,32768]{2,1,0:T(1,128)S(1)} %all-to-all-done.1, f32[]{:T(128)} %constant.176), dimensions={1}, to_apply=%all_to_all.27.reduce_sub_computation | reduce | bytes 2097156 | tf_op jit(solution)/shard_map/all_to_all | solution.py:96
  101.3 1.2 reshape.382.r_ref
  102.5 18.9 %shard_map.192 = (f32[2,64,4096]{2,1,0:T(8,128)}, f32[2,4,64,64]{3,2,1,0:T(8,128)}) custom-call(s32[6]{0:T(128)} %pad_add_fusion.sel_ref, f32[2,64,4096]{2,1,0:T(8,128)} %s_ref.1, f32[1,64,4096]{2,1,0:T(8,128)} %reshape.382.r_ref, f32[2,4,64,64]{3,2,1,0:T(8,128)} %broadcast_multiply_fusion.u_ref, f32[2,4,64,1]{3,2,1,0:T(8,128)} %copy.51.dec_ref, ...), custom_call_target="tpu_custom_call" | custom-call | tf_op jit(solution)/shard_map/pallas_call | solution.py:58
  121.4 1.1 multiply_add_fusion
  122.8 2.4 %psum.7 = f32[2,4]{1,0:T(2,128)S(1)} all-reduce(f32[2,4]{1,0:T(2,128)S(1)} %get-tuple-element.8), channel_id=1, replica_groups=mesh['parts'=2,'req'=8,'tp'=2] {'tp'}, use_global_device_ids=true, to_apply=%region_5.6 | all-reduce | flops 8 | bytes 64 | tf_op jit(solution)/shard_map/psum | solution.py:163
  125.3 0.7 multiply_convert_fusion
  (76 shorter events, 7.8 us)
Async XLA Ops:
  0.6 0.7 copy-start
  0.6 19.7 %copy-start.3 = (f32[4,4096]{1,0:T(4,128)S(1)}, f32[4,4096]{1,0:T(4,128)}, u32[]{:S(2)}) copy-start(f32[4,4096]{1,0:T(4,128)} %param.26) | copy-start | bytes 196612
  0.7 19.8 %copy-start.12 = (f32[64]{0:T(128)S(1)}, f32[64]{0:T(128)}, u32[]{:S(2)}) copy-start(f32[64]{0:T(128)} %param.31) | copy-start | bytes 772
  0.7 19.8 %copy-start.7 = (f32[4,2,128]{2,1,0:T(2,128)S(1)}, f32[4,2,128]{2,1,0:T(2,128)}, u32[]{:S(2)}) copy-start(f32[4,2,128]{2,1,0:T(2,128)} %param.28) | copy-start | bytes 12292
  0.7 19.8 %copy-start.1 = (bf16[2,4,4096]{2,1,0:T(4,128)(2,1)S(1)}, bf16[2,4,4096]{2,1,0:T(4,128)(2,1)}, u32[]{:S(2)}) copy-start(bf16[2,4,4096]{2,1,0:T(4,128)(2,1)} %param.22) | copy-start | bytes 196612
  0.7 20.6 %copy-start.6 = (bf16[2,4,2,128]{3,2,1,0:T(2,128)(2,1)S(1)}, bf16[2,4,2,128]{3,2,1,0:T(2,128)(2,1)}, u32[]{:S(2)}) copy-start(bf16[2,4,2,128]{3,2,1,0:T(2,128)(2,1)} %param.23) | copy-start | bytes 12292
  0.7 21.2 %copy-start.8 = (f32[2,4,64]{2,1,0:T(4,128)S(1)}, f32[2,4,64]{2,1,0:T(4,128)}, u32[]{:S(2)}) copy-start(f32[2,4,64]{2,1,0:T(4,128)} %param.25) | copy-start | bytes 6148
  0.7 21.2 %copy-start.10 = (f32[64]{0:T(128)S(1)}, f32[64]{0:T(128)}, u32[]{:S(2)}) copy-start(f32[64]{0:T(128)} %param.30) | copy-start | bytes 772
  9.0 13.9 %all-to-all-start.2 = ((bf16[8,2,816]{2,1,0:T(2,128)(2,1)}), bf16[8,2,816]{2,1,0:T(2,128)(2,1)S(1)}, u32[]{:S(2)}, u32[]{:S(2)}) async-start(bf16[8,2,816]{2,1,0:T(2,128)(2,1)} %reshape.424), calls=%async_computation.2 | async-start | bytes 57344 | tf_op jit(solution)/shard_map/all_to_all | solution.py:91
  25.1 11.7 %all-to-all-start.3 = ((bf16[8,2,816]{2,1,0:T(2,128)(2,1)}), bf16[8,2,816]{2,1,0:T(2,128)(2,1)S(1)}, u32[]{:S(2)}, u32[]{:S(2)}) async-start(bf16[8,2,816]{2,1,0:T(2,128)(2,1)} %reshape.426), calls=%async_computation.3 | async-start | bytes 57344 | tf_op jit(solution)/shard_map/all_to_all | solution.py:97
  36.8 28.5 %all-to-all-start = ((f32[8,1,32768]{2,1,0:T(1,128)}), f32[8,1,32768]{2,1,0:T(1,128)S(1)}, u32[]{:S(2)}, u32[]{:S(2)}) async-start(f32[8,1,32768]{2,1,0:T(1,128)} %all_to_all.24), calls=%async_computation | async-start | bytes 2097152 | tf_op jit(solution)/shard_map/all_to_all | solution.py:88
  67.0 6.0 %copy-start.4 = (f32[4096]{0:T(1024)S(1)}, f32[4096]{0:T(1024)}, u32[]{:S(2)}) copy-start(f32[4096]{0:T(1024)} %param.27) | copy-start | bytes 49156
  69.1 4.4 %copy-start.9 = (f32[2,128]{1,0:T(2,128)S(1)}, f32[2,128]{1,0:T(2,128)}, u32[]{:S(2)}) copy-start(f32[2,128]{1,0:T(2,128)} %param.29) | copy-start | bytes 3076
  69.1 29.6 %all-to-all-start.1 = ((f32[8,1,32768]{2,1,0:T(1,128)}), f32[8,1,32768]{2,1,0:T(1,128)S(1)}, u32[]{:S(2)}, u32[]{:S(2)}) async-start(f32[8,1,32768]{2,1,0:T(1,128)} %copy.45), calls=%async_computation.1 | async-start | bytes 2097152 | tf_op jit(solution)/shard_map/all_to_all | solution.py:96
  102.5 19.0 %copy-start.11 = (f32[64]{0:T(128)S(1)}, f32[64]{0:T(128)}, u32[]{:S(2)}) copy-start(f32[64]{0:T(128)} %param.32) | copy-start | bytes 772
  102.5 20.1 %copy-start.2 = (bf16[2,4,4096]{2,1,0:T(4,128)(2,1)S(1)}, bf16[2,4,4096]{2,1,0:T(4,128)(2,1)}, u32[]{:S(2)}) copy-start(bf16[2,4,4096]{2,1,0:T(4,128)(2,1)} %param.24) | copy-start | bytes 196612
  102.5 22.8 %copy-start.5 = (f32[4096]{0:T(1024)S(1)}, f32[4096]{0:T(1024)}, u32[]{:S(2)}) copy-start(f32[4096]{0:T(1024)} %param.33) | copy-start | bytes 49156

commit v3 on v2

--- a/solution.py
+++ b/solution.py
@@ -85,18 +85,15 @@
     src_owner = jnp.sum(jnp.where(incoming, ids[None, :], 0), axis=1) // slots
     out_state = lax.dynamic_index_in_dim(ssm_state, send_j, 0, keepdims=False)
     out_conv = lax.dynamic_index_in_dim(conv_flat, send_j, 0, keepdims=False)
-    spread_state = lax.all_to_all(
-        out_state.reshape(owners, -1), "req", split_axis=0, concat_axis=0, tiled=True
-    )
-    spread_conv = lax.all_to_all(
-        out_conv.reshape(owners, -1), "req", split_axis=0, concat_axis=0, tiled=True
-    )
-    picked_state = jnp.take(spread_state, src_owner, axis=0)
-    picked_conv = jnp.take(spread_conv, src_owner, axis=0)
-    rstate = lax.all_to_all(picked_state, "req", split_axis=0, concat_axis=0, tiled=True)
-    rconv = lax.all_to_all(picked_conv, "req", split_axis=0, concat_axis=0, tiled=True)
-    rstate = rstate.reshape((1,) + ssm_state.shape[1:])
-    rconv = rconv.reshape(1, -1)
+    state_words = out_state.reshape(owners, -1)
+    conv_words = out_conv.astype(jnp.float32).reshape(owners, -1)
+    split = state_words.shape[1]
+    packed = jnp.concatenate([state_words, conv_words], 1)
+    spread = lax.all_to_all(packed, "req", split_axis=0, concat_axis=0, tiled=True)
+    picked = jnp.take(spread, src_owner, axis=0)
+    arrived = lax.all_to_all(picked, "req", split_axis=0, concat_axis=0, tiled=True)
+    rstate = arrived[:, :split].reshape((1,) + ssm_state.shape[1:])
+    rconv = arrived[:, split:].astype(jnp.bfloat16).reshape(1, -1)
     targets = owner * slots + jnp.arange(slots, dtype=jnp.int32)
     match = live[None, :] & (move_plan[None, :] == targets[:, None])
     hit = jnp.any(match, axis=1)

time: 127 us -> 108 us (0.85)
  starting transfers between devices: 19.8 us -> 11.2 us
  other arithmetic: 14.7 us -> 7.64 us
  local copies, waits for them, and re-layouts: 17.2 us -> 14.1 us
    all_to_all x4 -> x2, starting transfers between devices: 19.8 us -> 11.2 us  [the longest x1 7.42 us: migrate(): lax.all_to_all(packed, 'req', split_axis=0, concat_axis=0, tiled=True)]
    all_to_all x3 -> x0, other arithmetic: 3.55 us -> none  [the longest x1 2.61 us: migrate(): lax.all_to_all(picked_state, 'req', split_axis=0, concat_axis=0, tiled=True)]
    unnamed x32 -> x36, local copies, waits for them, and re-layouts: 2.85 us -> 1.41 us
    all_to_all x3 -> x1, local copies, waits for them, and re-layouts: 2.83 us -> 1.74 us  [migrate(): lax.all_to_all(packed, 'req', split_axis=0, concat_axis=0, tiled=True)]
    all_to_all x4 -> x2, waiting for transfers between devices: 49.9 us -> 49.6 us  [the longest x1 25.5 us: migrate(): lax.all_to_all(packed, 'req', split_axis=0, concat_axis=0, tiled=True)]
  transfers between devices with their start and end apart: 4 -> 2, of which waited for: 4 -> 2; matrix products, arithmetic and copies ran while one was open for 9% -> 4% of each run, Pallas kernels for 0% -> 0%
where the time goes in v3:
time: 108 us; the launch traced here: 107 us
  waiting for transfers between devices  49.6 us (46%)
  Pallas kernels  19 us (18%)
  local copies, waits for them, and re-layouts  14.1 us (13%)
  starting transfers between devices  11.2 us (10%)
  other arithmetic  7.64 us (7%)
  between operations  2.98 us (3%)
  blocking collectives  2.45 us (2%)
    all_to_all x1, waiting for transfers between devices, migrate(): lax.all_to_all(packed, 'req', split_axis=0, concat_axis=0, tiled=True)  25.5 us
    all_to_all x1, waiting for transfers between devices, migrate(): lax.all_to_all(picked, 'req', split_axis=0, concat_axis=0, tiled=True)  24.1 us
    pallas_call x1, Pallas kernels, ssm_steps(): pl.pallas_call(ssm_kernel, grid_spec=grid_spec, out_shape=[jax.ShapeDtype...  19 us
    all_to_all x1, starting transfers between devices, migrate(): lax.all_to_all(packed, 'req', split_axis=0, concat_axis=0, tiled=True)  7.42 us
    all_to_all x1, starting transfers between devices, migrate(): lax.all_to_all(picked, 'req', split_axis=0, concat_axis=0, tiled=True)  3.77 us
    psum x1, blocking collectives, on_device(): total = lax.psum(jnp.sum(gated * gated, axis=-1), 'tp')  2.45 us
  transfers between devices with their start and end apart: 2, of which 2 were waited for; matrix products, arithmetic and copies ran while one was open for 4% of the time, Pallas kernels for 0%

profile of v3, /device:TPU:0, one launch (start us, length us, event | category | flops | bytes accessed | tf_op | source)
XLA Modules:
  0.0 107.0 jit_solution(8368872718399143800)
XLA Ops:
  0.7 0.6 copy-done
  1.3 0.7 gather_fusion
  1.9 1.3 %fusion.23 = (s32[]{:T(128)}, s32[16]{0:T(128)S(1)}, pred[16]{0:T(512)(128)(4,1)S(1)}, s32[16]{0:T(128)S(1)}) fusion(s32[]{:T(128)S(6)} %axis_index.15, s32[16]{0:T(128)} %param.18, s32[16]{0:T(128)S(1)} %gather_fusion), kind=kLoop, calls=%fused_computation.119 | loop fusion | flops 655 | bytes 280 | tf_op jit(solution)/shard_map/reduce_sum | solution.py:78
  5.2 1.3 %constant_dynamic-slice_fusion = f32[1,64,4096]{2,1,0:T(8,128)S(1)} fusion(f32[2,64,4096]{2,1,0:T(8,128)} %s_ref.1, s32[]{:T(128)S(6)} %select_n.236), kind=kLoop, calls=%fused_computation.109 | loop fusion | bytes 2097156 | tf_op jit(solution)/shard_map/jit(dynamic_index_in_dim)/dynamic_slice | solution.py:86
  6.5 0.2 reshape.355
  6.7 0.5 copy-done.12
  7.7 1.7 %all_to_all.14 = f32[8,1,34400]{2,1,0:T(1,128)} reshape(f32[8,34400]{1,0:T(8,128)S(1)} %pad_maximum_fusion) | data formatting | bytes 2201600 | tf_op jit(solution)/shard_map/all_to_all | solution.py:92
  9.5 7.4 %all-to-all-start = ((f32[8,1,34400]{2,1,0:T(1,128)}), f32[8,1,34400]{2,1,0:T(1,128)S(1)}, u32[]{:S(2)}, u32[]{:S(2)}) async-start(f32[8,1,34400]{2,1,0:T(1,128)} %all_to_all.14), calls=%async_computation | async-start | bytes 2203648 | tf_op jit(solution)/shard_map/all_to_all | solution.py:92
  17.1 0.2 fusion.18
  17.3 0.2 fusion.17
  17.6 0.7 broadcast_select_fusion.3
  18.3 25.5 %all-to-all-done = f32[8,1,34400]{2,1,0:T(1,128)S(1)} async-done(((f32[8,1,34400]{2,1,0:T(1,128)}), f32[8,1,34400]{2,1,0:T(1,128)S(1)}, u32[]{:S(2)}, u32[]{:S(2)}) %all-to-all-start) | async-done | bytes 1100832 | tf_op jit(solution)/shard_map/all_to_all | solution.py:92
  43.9 0.9 gather_fusion.1
  45.0 2.1 %copy.37 = f32[8,1,34400]{2,1,0:T(1,128)} copy(f32[8,1,34400]{2,0,1:T(8,128)S(1)} %bitcast_select_fusion) | data formatting | bytes 2201600 | tf_op jit(solution)/shard_map/jit(_take)/select_n | solution.py:93
  47.1 3.8 %all-to-all-start.1 = ((f32[8,1,34400]{2,1,0:T(1,128)}), f32[8,1,34400]{2,1,0:T(1,128)S(1)}, u32[]{:S(2)}, u32[]{:S(2)}) async-start(f32[8,1,34400]{2,1,0:T(1,128)} %copy.37), calls=%async_computation.1 | async-start | bytes 2203648 | tf_op jit(solution)/shard_map/all_to_all | solution.py:94
  50.9 0.9 copy.40.dec_ref
  51.8 0.6 gather_fusion.2
  52.4 0.6 pad_add_fusion.sel_ref
  53.0 0.7 broadcast_select_fusion.2
  53.8 24.1 %all-to-all-done.1 = f32[8,1,34400]{2,1,0:T(1,128)S(1)} async-done(((f32[8,1,34400]{2,1,0:T(1,128)}), f32[8,1,34400]{2,1,0:T(1,128)S(1)}, u32[]{:S(2)}, u32[]{:S(2)}) %all-to-all-start.1) | async-done | bytes 1100832 | tf_op jit(solution)/shard_map/all_to_all | solution.py:94
  78.4 1.2 %reshape.358.r_ref = f32[1,64,4096]{2,1,0:T(8,128)} reshape(f32[8,32768]{1,0:T(8,128)S(1)} %slice.103) | data formatting | bytes 2097152 | tf_op jit(solution)/shard_map/reshape | solution.py:95
  79.7 0.2 divide_multiply_fusion
  79.9 0.2 reshape.360
  80.1 0.3 slice-done
  80.6 0.9 tile.9
  81.6 0.9 tile.21
  82.5 0.8 broadcast_multiply_fusion.u_ref
  83.4 19.0 %shard_map.192 = (f32[2,64,4096]{2,1,0:T(8,128)}, f32[2,4,64,64]{3,2,1,0:T(8,128)}) custom-call(s32[6]{0:T(128)} %pad_add_fusion.sel_ref, f32[2,64,4096]{2,1,0:T(8,128)} %s_ref.1, f32[1,64,4096]{2,1,0:T(8,128)} %reshape.358.r_ref, f32[2,4,64,64]{3,2,1,0:T(8,128)} %broadcast_multiply_fusion.u_ref, f32[2,4,64,1]{3,2,1,0:T(8,128)} %copy.40.dec_ref, ...), custom_call_target="tpu_custom_call" | custom-call | tf_op jit(solution)/shard_map/pallas_call | solution.py:58
  102.3 1.1 %multiply_add_fusion = f32[2,4,64,64]{3,2,1,0:T(8,128)S(1)} fusion(f32[2,4,64,64]{3,2,1,0:T(8,128)} %get-tuple-element.6, f32[2,4,64,64]{3,2,1,0:T(8,128)S(1)} %reshape.360, f32[64]{0:T(128)S(1)} %copy-done.15), kind=kLoop, calls=%fused_computation.7 | loop fusion | flops 65536 | bytes 393472 | tf_op jit(solution)/shard_map/add | solution.py:158
  103.6 0.2 multiply_reduce_fusion
  103.8 2.4 %psum.7 = f32[2,4]{1,0:T(2,128)S(1)} all-reduce(f32[2,4]{1,0:T(2,128)S(1)} %get-tuple-element.8), channel_id=1, replica_groups=mesh['parts'=2,'req'=8,'tp'=2] {'tp'}, use_global_device_ids=true, to_apply=%region_5.6 | all-reduce | flops 8 | bytes 64 | tf_op jit(solution)/shard_map/psum | solution.py:160
  106.2 0.7 multiply_convert_fusion
  (74 shorter events, 2.0 us)
Async XLA Ops:
  0.6 0.7 copy-start
  6.5 0.7 copy-start.12
  6.5 0.8 copy-start.3
  9.4 7.6 %copy-start.9 = (s32[16]{0:T(128)S(1)}, s32[16]{0:T(128)}, u32[]{:S(2)}) copy-start(s32[16]{0:T(128)} %param.18) | copy-start | bytes 196
  9.4 8.1 %copy-start.10 = (f32[4,2,128]{2,1,0:T(2,128)S(1)}, f32[4,2,128]{2,1,0:T(2,128)}, u32[]{:S(2)}) copy-start(f32[4,2,128]{2,1,0:T(2,128)} %param.28) | copy-start | bytes 12292
  9.4 8.1 %copy-start.16 = (f32[64]{0:T(128)S(1)}, f32[64]{0:T(128)}, u32[]{:S(2)}) copy-start(f32[64]{0:T(128)} %param.31) | copy-start | bytes 772
  9.4 8.1 %copy-start.8 = (bf16[2,4,2,128]{3,2,1,0:T(2,128)(2,1)S(1)}, bf16[2,4,2,128]{3,2,1,0:T(2,128)(2,1)}, u32[]{:S(2)}) copy-start(bf16[2,4,2,128]{3,2,1,0:T(2,128)(2,1)} %param.23) | copy-start | bytes 12292
  9.5 8.8 %copy-start.11 = (f32[2,4,64]{2,1,0:T(4,128)S(1)}, f32[2,4,64]{2,1,0:T(4,128)}, u32[]{:S(2)}) copy-start(f32[2,4,64]{2,1,0:T(4,128)} %param.25) | copy-start | bytes 6148
  9.5 8.8 %copy-start.14 = (f32[64]{0:T(128)S(1)}, f32[64]{0:T(128)}, u32[]{:S(2)}) copy-start(f32[64]{0:T(128)} %param.30) | copy-start | bytes 772
  9.5 34.3 %all-to-all-start = ((f32[8,1,34400]{2,1,0:T(1,128)}), f32[8,1,34400]{2,1,0:T(1,128)S(1)}, u32[]{:S(2)}, u32[]{:S(2)}) async-start(f32[8,1,34400]{2,1,0:T(1,128)} %all_to_all.14), calls=%async_computation | async-start | bytes 2203648 | tf_op jit(solution)/shard_map/all_to_all | solution.py:92
  47.1 4.7 %copy-start.1 = (bf16[2,4,4096]{2,1,0:T(4,128)(2,1)S(1)}, bf16[2,4,4096]{2,1,0:T(4,128)(2,1)}, u32[]{:S(2)}) copy-start(bf16[2,4,4096]{2,1,0:T(4,128)(2,1)} %param.22) | copy-start | bytes 196612
  47.1 6.7 %copy-start.5 = (f32[4,4096]{1,0:T(4,128)S(1)}, f32[4,4096]{1,0:T(4,128)}, u32[]{:S(2)}) copy-start(f32[4,4096]{1,0:T(4,128)} %param.26) | copy-start | bytes 196612
  47.1 30.9 %all-to-all-start.1 = ((f32[8,1,34400]{2,1,0:T(1,128)}), f32[8,1,34400]{2,1,0:T(1,128)S(1)}, u32[]{:S(2)}, u32[]{:S(2)}) async-start(f32[8,1,34400]{2,1,0:T(1,128)} %copy.37), calls=%async_computation.1 | async-start | bytes 2203648 | tf_op jit(solution)/shard_map/all_to_all | solution.py:94
  78.3 1.3 %copy-start.2 = (bf16[2,13056]{1,0:T(2,128)(2,1)}, bf16[2,13056]{1,0:T(2,128)(2,1)S(1)}, u32[]{:S(2)}) copy-start(bf16[2,13056]{1,0:T(2,128)(2,1)S(1)} %broadcast_select_fusion.1) | copy-start | bytes 156676
  78.4 1.3 %copy-start.6 = (f32[4096]{0:T(1024)S(1)}, f32[4096]{0:T(1024)}, u32[]{:S(2)}) copy-start(f32[4096]{0:T(1024)} %param.27) | copy-start | bytes 49156
  79.6 0.9 copy-start.13
  79.7 0.7 slice-start
  83.4 19.0 %copy-start.15 = (f32[64]{0:T(128)S(1)}, f32[64]{0:T(128)}, u32[]{:S(2)}) copy-start(f32[64]{0:T(128)} %param.32) | copy-start | bytes 772
  102.3 1.2 %copy-start.4 = (bf16[2,4,4096]{2,1,0:T(4,128)(2,1)S(1)}, bf16[2,4,4096]{2,1,0:T(4,128)(2,1)}, u32[]{:S(2)}) copy-start(bf16[2,4,4096]{2,1,0:T(4,128)(2,1)} %param.24) | copy-start | bytes 196612
  102.3 3.9 %copy-start.7 = (f32[4096]{0:T(1024)S(1)}, f32[4096]{0:T(1024)}, u32[]{:S(2)}) copy-start(f32[4096]{0:T(1024)} %param.33) | copy-start | bytes 49156

commit v4 on v3

--- a/solution.py
+++ b/solution.py
@@ -16,19 +16,23 @@
     rows, cols = s_ref.shape[1], s_ref.shape[2]
     seg = u_ref.shape[3]
     lane_seg = lax.broadcasted_iota(jnp.int32, (seg, cols), 1) // (cols // seg)
-    expand = (lane_seg == lax.broadcasted_iota(jnp.int32, (seg, cols), 0)).astype(jnp.float32)
+    expand = (lane_seg == lax.broadcasted_iota(jnp.int32, (seg, cols), 0)).astype(jnp.bfloat16)
     state = jnp.where(sel_ref[places + k] == 1, r_ref[0], s_ref[0])
     for t in range(STEPS):
-        upd = jnp.dot(
-            u_ref[0, t], expand, precision=lax.Precision.HIGHEST,
-            preferred_element_type=jnp.float32,
+        u = u_ref[0, t]
+        u_hi = u.astype(jnp.bfloat16)
+        u_lo = (u - u_hi.astype(jnp.float32)).astype(jnp.bfloat16)
+        upd = jnp.dot(u_hi, expand, preferred_element_type=jnp.float32) + jnp.dot(
+            u_lo, expand, preferred_element_type=jnp.float32
         )
         state = dec_ref[0, t] * state + upd * b_ref[0, 0, t:t + 1, :]
         prod = state * c_ref[0, 0, t:t + 1, :]
+        p_hi = prod.astype(jnp.bfloat16)
+        p_lo = (prod - p_hi.astype(jnp.float32)).astype(jnp.bfloat16)
+        dims = (((1,), (1,)), ((), ()))
         y_ref[0, t] = lax.dot_general(
-            prod, expand, (((1,), (1,)), ((), ())), precision=lax.Precision.HIGHEST,
-            preferred_element_type=jnp.float32,
-        )
+            p_hi, expand, dims, preferred_element_type=jnp.float32
+        ) + lax.dot_general(p_lo, expand, dims, preferred_element_type=jnp.float32)
     keep = (sel_ref[2 * places + k] == 1).astype(jnp.float32)
     out_ref[0] = state * keep
 

time: 108 us -> 98 us (0.907)
  Pallas kernels: 19 us -> 9.49 us
    pallas_call x1, Pallas kernels: 19 us -> 9.49 us  [ssm_steps(): pl.pallas_call(ssm_kernel, grid_spec=grid_spec, out_shape=[jax.ShapeDtype...]
where the time goes in v4:
time: 98 us; the launch traced here: 97.5 us
  waiting for transfers between devices  49.6 us (51%)
  local copies, waits for them, and re-layouts  14.1 us (14%)
  starting transfers between devices  11.2 us (11%)
  Pallas kernels  9.49 us (10%)
  other arithmetic  7.64 us (8%)
  between operations  2.98 us (3%)
  blocking collectives  2.45 us (3%)
    all_to_all x1, waiting for transfers between devices, migrate(): lax.all_to_all(packed, 'req', split_axis=0, concat_axis=0, tiled=True)  25.5 us
    all_to_all x1, waiting for transfers between devices, migrate(): lax.all_to_all(picked, 'req', split_axis=0, concat_axis=0, tiled=True)  24.1 us
    pallas_call x1, Pallas kernels, ssm_steps(): pl.pallas_call(ssm_kernel, grid_spec=grid_spec, out_shape=[jax.ShapeDtype...  9.49 us
    all_to_all x1, starting transfers between devices, migrate(): lax.all_to_all(packed, 'req', split_axis=0, concat_axis=0, tiled=True)  7.42 us
    all_to_all x1, starting transfers between devices, migrate(): lax.all_to_all(picked, 'req', split_axis=0, concat_axis=0, tiled=True)  3.77 us
    psum x1, blocking collectives, on_device(): total = lax.psum(jnp.sum(gated * gated, axis=-1), 'tp')  2.45 us
    select_n x1, local copies, waits for them, and re-layouts, migrate(): picked = jnp.take(spread, src_owner, axis=0)  2.12 us
  transfers between devices with their start and end apart: 2, of which 2 were waited for; matrix products, arithmetic and copies ran while one was open for 4% of the time, Pallas kernels for 0%

profile of v4, /device:TPU:0, one launch (start us, length us, event | category | flops | bytes accessed | tf_op | source)
XLA Modules:
  0.0 97.5 jit_solution(15647655163557491943)
XLA Ops:
  0.7 0.6 copy-done
  1.3 0.7 gather_fusion
  1.9 1.3 %fusion.23 = (s32[]{:T(128)}, s32[16]{0:T(128)S(1)}, pred[16]{0:T(512)(128)(4,1)S(1)}, s32[16]{0:T(128)S(1)}) fusion(s32[]{:T(128)S(6)} %axis_index.15, s32[16]{0:T(128)} %param.18, s32[16]{0:T(128)S(1)} %gather_fusion), kind=kLoop, calls=%fused_computation.119 | loop fusion | flops 655 | bytes 280 | tf_op jit(solution)/shard_map/reduce_sum | solution.py:82
  5.2 1.3 %constant_dynamic-slice_fusion = f32[1,64,4096]{2,1,0:T(8,128)S(1)} fusion(f32[2,64,4096]{2,1,0:T(8,128)} %s_ref.1, s32[]{:T(128)S(6)} %select_n.236), kind=kLoop, calls=%fused_computation.109 | loop fusion | bytes 2097156 | tf_op jit(solution)/shard_map/jit(dynamic_index_in_dim)/dynamic_slice | solution.py:90
  6.5 0.2 reshape.355
  6.7 0.5 copy-done.12
  7.7 1.7 %all_to_all.14 = f32[8,1,34400]{2,1,0:T(1,128)} reshape(f32[8,34400]{1,0:T(8,128)S(1)} %pad_maximum_fusion) | data formatting | bytes 2201600 | tf_op jit(solution)/shard_map/all_to_all | solution.py:96
  9.5 7.4 %all-to-all-start = ((f32[8,1,34400]{2,1,0:T(1,128)}), f32[8,1,34400]{2,1,0:T(1,128)S(1)}, u32[]{:S(2)}, u32[]{:S(2)}) async-start(f32[8,1,34400]{2,1,0:T(1,128)} %all_to_all.14), calls=%async_computation | async-start | bytes 2203648 | tf_op jit(solution)/shard_map/all_to_all | solution.py:96
  17.1 0.2 fusion.18
  17.3 0.2 fusion.17
  17.6 0.7 broadcast_select_fusion.3
  18.3 25.5 %all-to-all-done = f32[8,1,34400]{2,1,0:T(1,128)S(1)} async-done(((f32[8,1,34400]{2,1,0:T(1,128)}), f32[8,1,34400]{2,1,0:T(1,128)S(1)}, u32[]{:S(2)}, u32[]{:S(2)}) %all-to-all-start) | async-done | bytes 1100832 | tf_op jit(solution)/shard_map/all_to_all | solution.py:96
  43.9 0.9 gather_fusion.1
  45.0 2.1 %copy.37 = f32[8,1,34400]{2,1,0:T(1,128)} copy(f32[8,1,34400]{2,0,1:T(8,128)S(1)} %bitcast_select_fusion) | data formatting | bytes 2201600 | tf_op jit(solution)/shard_map/jit(_take)/select_n | solution.py:97
  47.1 3.8 %all-to-all-start.1 = ((f32[8,1,34400]{2,1,0:T(1,128)}), f32[8,1,34400]{2,1,0:T(1,128)S(1)}, u32[]{:S(2)}, u32[]{:S(2)}) async-start(f32[8,1,34400]{2,1,0:T(1,128)} %copy.37), calls=%async_computation.1 | async-start | bytes 2203648 | tf_op jit(solution)/shard_map/all_to_all | solution.py:98
  50.9 0.9 copy.40.dec_ref
  51.8 0.6 gather_fusion.2
  52.4 0.6 pad_add_fusion.sel_ref
  53.0 0.7 broadcast_select_fusion.2
  53.8 24.1 %all-to-all-done.1 = f32[8,1,34400]{2,1,0:T(1,128)S(1)} async-done(((f32[8,1,34400]{2,1,0:T(1,128)}), f32[8,1,34400]{2,1,0:T(1,128)S(1)}, u32[]{:S(2)}, u32[]{:S(2)}) %all-to-all-start.1) | async-done | bytes 1100832 | tf_op jit(solution)/shard_map/all_to_all | solution.py:98
  78.4 1.2 %reshape.358.r_ref = f32[1,64,4096]{2,1,0:T(8,128)} reshape(f32[8,32768]{1,0:T(8,128)S(1)} %slice.103) | data formatting | bytes 2097152 | tf_op jit(solution)/shard_map/reshape | solution.py:99
  79.7 0.2 divide_multiply_fusion
  79.9 0.2 reshape.360
  80.1 0.3 slice-done
  80.6 0.9 tile.9
  81.6 0.9 tile.21
  82.5 0.8 broadcast_multiply_fusion.u_ref
  83.4 9.5 %shard_map.192 = (f32[2,64,4096]{2,1,0:T(8,128)}, f32[2,4,64,64]{3,2,1,0:T(8,128)}) custom-call(s32[6]{0:T(128)} %pad_add_fusion.sel_ref, f32[2,64,4096]{2,1,0:T(8,128)} %s_ref.1, f32[1,64,4096]{2,1,0:T(8,128)} %reshape.358.r_ref, f32[2,4,64,64]{3,2,1,0:T(8,128)} %broadcast_multiply_fusion.u_ref, f32[2,4,64,1]{3,2,1,0:T(8,128)} %copy.40.dec_ref, ...), custom_call_target="tpu_custom_call" | custom-call | tf_op jit(solution)/shard_map/pallas_call | solution.py:62
  92.9 1.1 %multiply_add_fusion = f32[2,4,64,64]{3,2,1,0:T(8,128)S(1)} fusion(f32[2,4,64,64]{3,2,1,0:T(8,128)} %get-tuple-element.6, f32[2,4,64,64]{3,2,1,0:T(8,128)S(1)} %reshape.360, f32[64]{0:T(128)S(1)} %copy-done.15), kind=kLoop, calls=%fused_computation.7 | loop fusion | flops 65536 | bytes 393472 | tf_op jit(solution)/shard_map/add | solution.py:162
  94.1 0.2 multiply_reduce_fusion
  94.3 2.4 %psum.7 = f32[2,4]{1,0:T(2,128)S(1)} all-reduce(f32[2,4]{1,0:T(2,128)S(1)} %get-tuple-element.8), channel_id=1, replica_groups=mesh['parts'=2,'req'=8,'tp'=2] {'tp'}, use_global_device_ids=true, to_apply=%region_5.6 | all-reduce | flops 8 | bytes 64 | tf_op jit(solution)/shard_map/psum | solution.py:164
  96.8 0.7 multiply_convert_fusion
  (74 shorter events, 2.0 us)
Async XLA Ops:
  0.6 0.7 copy-start
  6.5 0.7 copy-start.12
  6.5 0.8 copy-start.3
  9.4 7.6 %copy-start.9 = (s32[16]{0:T(128)S(1)}, s32[16]{0:T(128)}, u32[]{:S(2)}) copy-start(s32[16]{0:T(128)} %param.18) | copy-start | bytes 196
  9.4 8.1 %copy-start.10 = (f32[4,2,128]{2,1,0:T(2,128)S(1)}, f32[4,2,128]{2,1,0:T(2,128)}, u32[]{:S(2)}) copy-start(f32[4,2,128]{2,1,0:T(2,128)} %param.28) | copy-start | bytes 12292
  9.4 8.1 %copy-start.16 = (f32[64]{0:T(128)S(1)}, f32[64]{0:T(128)}, u32[]{:S(2)}) copy-start(f32[64]{0:T(128)} %param.31) | copy-start | bytes 772
  9.4 8.1 %copy-start.8 = (bf16[2,4,2,128]{3,2,1,0:T(2,128)(2,1)S(1)}, bf16[2,4,2,128]{3,2,1,0:T(2,128)(2,1)}, u32[]{:S(2)}) copy-start(bf16[2,4,2,128]{3,2,1,0:T(2,128)(2,1)} %param.23) | copy-start | bytes 12292
  9.5 8.8 %copy-start.11 = (f32[2,4,64]{2,1,0:T(4,128)S(1)}, f32[2,4,64]{2,1,0:T(4,128)}, u32[]{:S(2)}) copy-start(f32[2,4,64]{2,1,0:T(4,128)} %param.25) | copy-start | bytes 6148
  9.5 8.8 %copy-start.14 = (f32[64]{0:T(128)S(1)}, f32[64]{0:T(128)}, u32[]{:S(2)}) copy-start(f32[64]{0:T(128)} %param.30) | copy-start | bytes 772
  9.5 34.3 %all-to-all-start = ((f32[8,1,34400]{2,1,0:T(1,128)}), f32[8,1,34400]{2,1,0:T(1,128)S(1)}, u32[]{:S(2)}, u32[]{:S(2)}) async-start(f32[8,1,34400]{2,1,0:T(1,128)} %all_to_all.14), calls=%async_computation | async-start | bytes 2203648 | tf_op jit(solution)/shard_map/all_to_all | solution.py:96
  47.1 4.7 %copy-start.1 = (bf16[2,4,4096]{2,1,0:T(4,128)(2,1)S(1)}, bf16[2,4,4096]{2,1,0:T(4,128)(2,1)}, u32[]{:S(2)}) copy-start(bf16[2,4,4096]{2,1,0:T(4,128)(2,1)} %param.22) | copy-start | bytes 196612
  47.1 6.7 %copy-start.5 = (f32[4,4096]{1,0:T(4,128)S(1)}, f32[4,4096]{1,0:T(4,128)}, u32[]{:S(2)}) copy-start(f32[4,4096]{1,0:T(4,128)} %param.26) | copy-start | bytes 196612
  47.1 30.9 %all-to-all-start.1 = ((f32[8,1,34400]{2,1,0:T(1,128)}), f32[8,1,34400]{2,1,0:T(1,128)S(1)}, u32[]{:S(2)}, u32[]{:S(2)}) async-start(f32[8,1,34400]{2,1,0:T(1,128)} %copy.37), calls=%async_computation.1 | async-start | bytes 2203648 | tf_op jit(solution)/shard_map/all_to_all | solution.py:98
  78.3 1.3 %copy-start.2 = (bf16[2,13056]{1,0:T(2,128)(2,1)}, bf16[2,13056]{1,0:T(2,128)(2,1)S(1)}, u32[]{:S(2)}) copy-start(bf16[2,13056]{1,0:T(2,128)(2,1)S(1)} %broadcast_select_fusion.1) | copy-start | bytes 156676
  78.4 1.3 %copy-start.6 = (f32[4096]{0:T(1024)S(1)}, f32[4096]{0:T(1024)}, u32[]{:S(2)}) copy-start(f32[4096]{0:T(1024)} %param.27) | copy-start | bytes 49156
  79.6 0.9 copy-start.13
  79.7 0.7 slice-start
  83.4 9.5 %copy-start.15 = (f32[64]{0:T(128)S(1)}, f32[64]{0:T(128)}, u32[]{:S(2)}) copy-start(f32[64]{0:T(128)} %param.32) | copy-start | bytes 772
  92.9 1.2 %copy-start.4 = (bf16[2,4,4096]{2,1,0:T(4,128)(2,1)S(1)}, bf16[2,4,4096]{2,1,0:T(4,128)(2,1)}, u32[]{:S(2)}) copy-start(bf16[2,4,4096]{2,1,0:T(4,128)(2,1)} %param.24) | copy-start | bytes 196612
  92.9 3.9 %copy-start.7 = (f32[4096]{0:T(1024)S(1)}, f32[4096]{0:T(1024)}, u32[]{:S(2)}) copy-start(f32[4096]{0:T(1024)} %param.33) | copy-start | bytes 49156

commit v5 on v4

--- a/solution.py
+++ b/solution.py
@@ -93,9 +93,17 @@
     conv_words = out_conv.astype(jnp.float32).reshape(owners, -1)
     split = state_words.shape[1]
     packed = jnp.concatenate([state_words, conv_words], 1)
-    spread = lax.all_to_all(packed, "req", split_axis=0, concat_axis=0, tiled=True)
-    picked = jnp.take(spread, src_owner, axis=0)
-    arrived = lax.all_to_all(picked, "req", split_axis=0, concat_axis=0, tiled=True)
+    half = packed.shape[1] // 2
+    chunks = [packed[:, :half], packed[:, half:]]
+    spreads = [
+        lax.all_to_all(c, "req", split_axis=0, concat_axis=0, tiled=True) for c in chunks
+    ]
+    arrived = jnp.concatenate([
+        lax.all_to_all(
+            jnp.take(s, src_owner, axis=0), "req", split_axis=0, concat_axis=0, tiled=True
+        )
+        for s in spreads
+    ], 1)
     rstate = arrived[:, :split].reshape((1,) + ssm_state.shape[1:])
     rconv = arrived[:, split:].astype(jnp.bfloat16).reshape(1, -1)
     targets = owner * slots + jnp.arange(slots, dtype=jnp.int32)

time: 98 us -> 110 us (1.12)
  starting transfers between devices: 11.2 us -> 18.2 us
  waiting for transfers between devices: 49.6 us -> 52.9 us
  local copies, waits for them, and re-layouts: 14.1 us -> 15.3 us
    all_to_all x2 -> x4, starting transfers between devices: 11.2 us -> 18.2 us  [the longest x2 10.9 us: migrate(): lax.all_to_all(c, 'req', split_axis=0, concat_axis=0, tiled=True)]
    all_to_all x1 -> x4, local copies, waits for them, and re-layouts: 1.74 us -> 5.3 us  [the longest x2 2.75 us: migrate(): lax.all_to_all(jnp.take(s, src_owner, axis=0), 'req', split_axis=0, conca...]
    all_to_all x2 -> x4, waiting for transfers between devices: 49.6 us -> 52.9 us  [the longest x2 28.1 us: migrate(): lax.all_to_all(jnp.take(s, src_owner, axis=0), 'req', split_axis=0, conca...]
    select_n x1 -> x0, local copies, waits for them, and re-layouts: 2.12 us -> none  [migrate(): picked = jnp.take(spread, src_owner, axis=0)]
  transfers between devices with their start and end apart: 2 -> 4, of which waited for: 2 -> 4; matrix products, arithmetic and copies ran while one was open for 4% -> 6% of each run, Pallas kernels for 0% -> 0%
where the time goes in v5:
time: 110 us; the launch traced here: 109 us
  waiting for transfers between devices  52.9 us (48%)
  starting transfers between devices  18.2 us (17%)
  local copies, waits for them, and re-layouts  15.3 us (14%)
  Pallas kernels  9.49 us (9%)
  other arithmetic  7.92 us (7%)
  between operations  3.01 us (3%)
  blocking collectives  2.45 us (2%)
    all_to_all x2, waiting for transfers between devices, migrate(): lax.all_to_all(jnp.take(s, src_owner, axis=0), 'req', split_axis=0, conca...  28.1 us
    all_to_all x2, waiting for transfers between devices, migrate(): lax.all_to_all(c, 'req', split_axis=0, concat_axis=0, tiled=True)  24.7 us
    all_to_all x2, starting transfers between devices, migrate(): lax.all_to_all(c, 'req', split_axis=0, concat_axis=0, tiled=True)  10.9 us
    pallas_call x1, Pallas kernels, ssm_steps(): pl.pallas_call(ssm_kernel, grid_spec=grid_spec, out_shape=[jax.ShapeDtype...  9.49 us
    all_to_all x2, starting transfers between devices, migrate(): lax.all_to_all(jnp.take(s, src_owner, axis=0), 'req', split_axis=0, conca...  7.27 us
    all_to_all x2, local copies, waits for them, and re-layouts, migrate(): lax.all_to_all(jnp.take(s, src_owner, axis=0), 'req', split_axis=0, conca...  2.75 us
    all_to_all x2, local copies, waits for them, and re-layouts, migrate(): lax.all_to_all(c, 'req', split_axis=0, concat_axis=0, tiled=True)  2.56 us
    psum x1, blocking collectives, on_device(): total = lax.psum(jnp.sum(gated * gated, axis=-1), 'tp')  2.45 us
  transfers between devices with their start and end apart: 4, of which 4 were waited for; matrix products, arithmetic and copies ran while one was open for 6% of the time, Pallas kernels for 0%

profile of v5, /device:TPU:0, one launch (start us, length us, event | category | flops | bytes accessed | tf_op | source)
XLA Modules:
  0.0 109.2 jit_solution(5503311277628311237)
XLA Ops:
  0.7 0.6 copy-done
  1.3 0.7 gather_fusion
  1.9 1.3 %fusion.23 = (s32[]{:T(128)}, s32[16]{0:T(128)S(1)}, pred[16]{0:T(512)(128)(4,1)S(1)}, s32[16]{0:T(128)S(1)}) fusion(s32[]{:T(128)S(6)} %axis_index.15, s32[16]{0:T(128)} %param.20, s32[16]{0:T(128)S(1)} %gather_fusion), kind=kLoop, calls=%fused_computation.118 | loop fusion | flops 655 | bytes 280 | tf_op jit(solution)/shard_map/reduce_sum | solution.py:82
  5.2 1.3 %constant_dynamic-slice_fusion = f32[1,64,4096]{2,1,0:T(8,128)S(1)} fusion(f32[2,64,4096]{2,1,0:T(8,128)} %s_ref.1, s32[]{:T(128)S(6)} %select_n.202), kind=kLoop, calls=%fused_computation.110 | loop fusion | bytes 2097156 | tf_op jit(solution)/shard_map/jit(dynamic_index_in_dim)/dynamic_slice | solution.py:90
  7.1 0.2 fusion.26
  7.4 1.4 %copy.40 = f32[8,1,17200]{2,1,0:T(1,128)} copy(f32[8,1,17200]{2,0,1:T(8,128)S(1)} %get-tuple-element.22) | data formatting | bytes 1100800 | tf_op jit(solution)/shard_map/all_to_all | solution.py:99
  8.7 7.3 %all-to-all-start.2 = ((f32[8,1,17200]{2,1,0:T(1,128)}), f32[8,1,17200]{2,1,0:T(1,128)S(1)}, u32[]{:S(2)}, u32[]{:S(2)}) async-start(f32[8,1,17200]{2,1,0:T(1,128)} %copy.40), calls=%async_computation.2 | async-start | bytes 1105920 | tf_op jit(solution)/shard_map/all_to_all | solution.py:99
  16.6 1.2 %all_to_all.32 = f32[8,1,17200]{2,1,0:T(1,128)} reshape(f32[8,17200]{1,0:T(8,128)S(1)} %get-tuple-element.21) | data formatting | bytes 1100800 | tf_op jit(solution)/shard_map/all_to_all | solution.py:99
  17.8 0.9 copy.44.dec_ref
  18.7 0.6 gather_fusion.1
  19.5 0.7 broadcast_select_fusion.3
  20.2 11.0 %all-to-all-done.2 = f32[8,1,17200]{2,1,0:T(1,128)S(1)} async-done(((f32[8,1,17200]{2,1,0:T(1,128)}), f32[8,1,17200]{2,1,0:T(1,128)S(1)}, u32[]{:S(2)}, u32[]{:S(2)}) %all-to-all-start.2) | async-done | bytes 550432 | tf_op jit(solution)/shard_map/all_to_all | solution.py:99
  31.1 3.6 %all-to-all-start = ((f32[8,1,17200]{2,1,0:T(1,128)}), f32[8,1,17200]{2,1,0:T(1,128)S(1)}, u32[]{:S(2)}, u32[]{:S(2)}) async-start(f32[8,1,17200]{2,1,0:T(1,128)} %all_to_all.32), calls=%async_computation | async-start | bytes 1105920 | tf_op jit(solution)/shard_map/all_to_all | solution.py:99
  34.8 0.7 broadcast_select_fusion.2
  35.5 0.7 gather_fusion.3
  36.3 13.8 %all-to-all-done = f32[8,1,17200]{2,1,0:T(1,128)S(1)} async-done(((f32[8,1,17200]{2,1,0:T(1,128)}), f32[8,1,17200]{2,1,0:T(1,128)S(1)}, u32[]{:S(2)}, u32[]{:S(2)}) %all-to-all-start) | async-done | bytes 550432 | tf_op jit(solution)/shard_map/all_to_all | solution.py:99
  50.1 0.7 gather_fusion.2
  51.0 1.4 %copy.41 = f32[8,1,17200]{2,1,0:T(1,128)} copy(f32[8,1,17200]{2,0,1:T(8,128)S(1)} %get-tuple-element.40) | data formatting | bytes 1100800 | tf_op jit(solution)/shard_map/all_to_all | solution.py:102
  52.4 3.6 %all-to-all-start.3 = ((f32[8,1,17200]{2,1,0:T(1,128)}), f32[8,1,17200]{2,1,0:T(1,128)S(1)}, u32[]{:S(2)}, u32[]{:S(2)}) async-start(f32[8,1,17200]{2,1,0:T(1,128)} %copy.41), calls=%async_computation.3 | async-start | bytes 1105920 | tf_op jit(solution)/shard_map/all_to_all | solution.py:102
  56.0 0.6 pad_add_fusion.sel_ref
  56.6 1.4 %copy.38 = f32[8,1,17200]{2,1,0:T(1,128)} copy(f32[8,1,17200]{2,0,1:T(8,128)S(1)} %get-tuple-element.39) | data formatting | bytes 1100800 | tf_op jit(solution)/shard_map/all_to_all | solution.py:102
  58.0 13.3 %all-to-all-done.3 = f32[8,1,17200]{2,1,0:T(1,128)S(1)} async-done(((f32[8,1,17200]{2,1,0:T(1,128)}), f32[8,1,17200]{2,1,0:T(1,128)S(1)}, u32[]{:S(2)}, u32[]{:S(2)}) %all-to-all-start.3) | async-done | bytes 550432 | tf_op jit(solution)/shard_map/all_to_all | solution.py:102
  71.3 3.6 %all-to-all-start.1 = ((f32[8,1,17200]{2,1,0:T(1,128)}), f32[8,1,17200]{2,1,0:T(1,128)S(1)}, u32[]{:S(2)}, u32[]{:S(2)}) async-start(f32[8,1,17200]{2,1,0:T(1,128)} %copy.38), calls=%async_computation.1 | async-start | bytes 1105920 | tf_op jit(solution)/shard_map/all_to_all | solution.py:102
  75.3 14.9 %all-to-all-done.1 = f32[8,1,17200]{2,1,0:T(1,128)S(1)} async-done(((f32[8,1,17200]{2,1,0:T(1,128)}), f32[8,1,17200]{2,1,0:T(1,128)S(1)}, u32[]{:S(2)}, u32[]{:S(2)}) %all-to-all-start.1) | async-done | bytes 550432 | tf_op jit(solution)/shard_map/all_to_all | solution.py:102
  90.5 1.2 %reshape.281.r_ref = f32[1,64,4096]{2,1,0:T(8,128)} reshape(f32[8,32768]{1,0:T(8,128)S(1)} %pad_maximum_fusion) | data formatting | bytes 2097152 | tf_op jit(solution)/shard_map/reshape | solution.py:107
  92.4 0.9 tile.9
  93.3 0.9 tile.21
  94.3 0.8 broadcast_multiply_fusion.u_ref
  95.1 9.5 %shard_map.192 = (f32[2,64,4096]{2,1,0:T(8,128)}, f32[2,4,64,64]{3,2,1,0:T(8,128)}) custom-call(s32[6]{0:T(128)} %pad_add_fusion.sel_ref, f32[2,64,4096]{2,1,0:T(8,128)} %s_ref.1, f32[1,64,4096]{2,1,0:T(8,128)} %reshape.281.r_ref, f32[2,4,64,64]{3,2,1,0:T(8,128)} %broadcast_multiply_fusion.u_ref, f32[2,4,64,1]{3,2,1,0:T(8,128)} %copy.44.dec_ref, ...), custom_call_target="tpu_custom_call" | custom-call | tf_op jit(solution)/shard_map/pallas_call | solution.py:62
  104.6 1.1 multiply_add_fusion
  106.0 2.4 %psum.7 = f32[2,4]{1,0:T(2,128)S(1)} all-reduce(f32[2,4]{1,0:T(2,128)S(1)} %get-tuple-element.9), channel_id=1, replica_groups=mesh['parts'=2,'req'=8,'tp'=2] {'tp'}, use_global_device_ids=true, to_apply=%region_5.7 | all-reduce | flops 8 | bytes 64 | tf_op jit(solution)/shard_map/psum | solution.py:172
  108.5 0.7 multiply_convert_fusion
  (79 shorter events, 3.2 us)
Async XLA Ops:
  0.6 0.7 copy-start
  5.2 1.5 %copy-start.11 = (bf16[2,3,2,128]{3,2,1,0:T(2,128)(2,1)S(1)}, bf16[2,3,2,128]{3,2,1,0:T(2,128)(2,1)}, u32[]{:S(2)}) copy-start(bf16[2,3,2,128]{3,2,1,0:T(2,128)(2,1)} %param.23) | copy-start | bytes 9220
  5.2 1.6 %copy-start.2 = (bf16[2,3,4096]{2,0,1:T(2,128)(2,1)S(1)}, bf16[2,3,4096]{2,0,1:T(2,128)(2,1)}, u32[]{:S(2)}) copy-start(bf16[2,3,4096]{2,0,1:T(2,128)(2,1)} %param.22) | copy-start | bytes 147460
  7.1 9.0 %copy-start.8 = (s32[16]{0:T(128)S(1)}, s32[16]{0:T(128)}, u32[]{:S(2)}) copy-start(s32[16]{0:T(128)} %param.20) | copy-start | bytes 196
  7.1 9.4 %copy-start.15 = (f32[64]{0:T(128)S(1)}, f32[64]{0:T(128)}, u32[]{:S(2)}) copy-start(f32[64]{0:T(128)} %param.33) | copy-start | bytes 772
  7.1 9.4 %copy-start.9 = (f32[2,4,64]{2,1,0:T(4,128)S(1)}, f32[2,4,64]{2,1,0:T(4,128)}, u32[]{:S(2)}) copy-start(f32[2,4,64]{2,1,0:T(4,128)} %param.27) | copy-start | bytes 6148
  7.1 9.4 %copy-start.13 = (f32[64]{0:T(128)S(1)}, f32[64]{0:T(128)}, u32[]{:S(2)}) copy-start(f32[64]{0:T(128)} %param.32) | copy-start | bytes 772
  7.3 11.3 %copy-start.1 = (bf16[2,4,4096]{2,1,0:T(4,128)(2,1)S(1)}, bf16[2,4,4096]{2,1,0:T(4,128)(2,1)}, u32[]{:S(2)}) copy-start(bf16[2,4,4096]{2,1,0:T(4,128)(2,1)} %param.24) | copy-start | bytes 196612
  7.3 12.1 %copy-start.10 = (f32[4,2,128]{2,1,0:T(2,128)S(1)}, f32[4,2,128]{2,1,0:T(2,128)}, u32[]{:S(2)}) copy-start(f32[4,2,128]{2,1,0:T(2,128)} %param.30) | copy-start | bytes 12292
  7.4 12.1 %copy-start.7 = (bf16[2,4,2,128]{3,2,1,0:T(2,128)(2,1)S(1)}, bf16[2,4,2,128]{3,2,1,0:T(2,128)(2,1)}, u32[]{:S(2)}) copy-start(bf16[2,4,2,128]{3,2,1,0:T(2,128)(2,1)} %param.25) | copy-start | bytes 12292
  8.7 22.4 %all-to-all-start.2 = ((f32[8,1,17200]{2,1,0:T(1,128)}), f32[8,1,17200]{2,1,0:T(1,128)S(1)}, u32[]{:S(2)}, u32[]{:S(2)}) async-start(f32[8,1,17200]{2,1,0:T(1,128)} %copy.40), calls=%async_computation.2 | async-start | bytes 1105920 | tf_op jit(solution)/shard_map/all_to_all | solution.py:99
  31.1 18.9 %all-to-all-start = ((f32[8,1,17200]{2,1,0:T(1,128)}), f32[8,1,17200]{2,1,0:T(1,128)S(1)}, u32[]{:S(2)}, u32[]{:S(2)}) async-start(f32[8,1,17200]{2,1,0:T(1,128)} %all_to_all.32), calls=%async_computation | async-start | bytes 1105920 | tf_op jit(solution)/shard_map/all_to_all | solution.py:99
  50.8 5.8 %copy-start.4 = (f32[4,4096]{1,0:T(4,128)S(1)}, f32[4,4096]{1,0:T(4,128)}, u32[]{:S(2)}) copy-start(f32[4,4096]{1,0:T(4,128)} %param.28) | copy-start | bytes 196612
  52.4 18.9 %all-to-all-start.3 = ((f32[8,1,17200]{2,1,0:T(1,128)}), f32[8,1,17200]{2,1,0:T(1,128)S(1)}, u32[]{:S(2)}, u32[]{:S(2)}) async-start(f32[8,1,17200]{2,1,0:T(1,128)} %copy.41), calls=%async_computation.3 | async-start | bytes 1105920 | tf_op jit(solution)/shard_map/all_to_all | solution.py:102
  71.3 18.9 %all-to-all-start.1 = ((f32[8,1,17200]{2,1,0:T(1,128)}), f32[8,1,17200]{2,1,0:T(1,128)S(1)}, u32[]{:S(2)}, u32[]{:S(2)}) async-start(f32[8,1,17200]{2,1,0:T(1,128)} %copy.38), calls=%async_computation.1 | async-start | bytes 1105920 | tf_op jit(solution)/shard_map/all_to_all | solution.py:102
  90.2 1.5 %copy-start.5 = (f32[4096]{0:T(1024)S(1)}, f32[4096]{0:T(1024)}, u32[]{:S(2)}) copy-start(f32[4096]{0:T(1024)} %param.29) | copy-start | bytes 49156
  90.5 1.7 %copy-start.12 = (f32[2,128]{1,0:T(2,128)S(1)}, f32[2,128]{1,0:T(2,128)}, u32[]{:S(2)}) copy-start(f32[2,128]{1,0:T(2,128)} %param.31) | copy-start | bytes 3076
  95.1 9.5 %copy-start.14 = (f32[64]{0:T(128)S(1)}, f32[64]{0:T(128)}, u32[]{:S(2)}) copy-start(f32[64]{0:T(128)} %param.34) | copy-start | bytes 772
  95.1 10.7 %copy-start.3 = (bf16[2,4,4096]{2,1,0:T(4,128)(2,1)S(1)}, bf16[2,4,4096]{2,1,0:T(4,128)(2,1)}, u32[]{:S(2)}) copy-start(bf16[2,4,4096]{2,1,0:T(4,128)(2,1)} %param.26) | copy-start | bytes 196612
  95.1 13.3 %copy-start.6 = (f32[4096]{0:T(1024)S(1)}, f32[4096]{0:T(1024)}, u32[]{:S(2)}) copy-start(f32[4096]{0:T(1024)} %param.35) | copy-start | bytes 49156

commit v6 on v4

--- a/solution.py
+++ b/solution.py
@@ -17,6 +17,21 @@
     seg = u_ref.shape[3]
     lane_seg = lax.broadcasted_iota(jnp.int32, (seg, cols), 1) // (cols // seg)
     expand = (lane_seg == lax.broadcasted_iota(jnp.int32, (seg, cols), 0)).astype(jnp.bfloat16)
+    nsz = b_ref.shape[3]
+    tiler = (
+        lax.broadcasted_iota(jnp.int32, (nsz, cols), 1) % nsz
+        == lax.broadcasted_iota(jnp.int32, (nsz, cols), 0)
+    ).astype(jnp.bfloat16)
+
+    def spread(v):
+        v_hi = v.astype(jnp.bfloat16)
+        v_lo = (v - v_hi.astype(jnp.float32)).astype(jnp.bfloat16)
+        return jnp.dot(v_hi, tiler, preferred_element_type=jnp.float32) + jnp.dot(
+            v_lo, tiler, preferred_element_type=jnp.float32
+        )
+
+    b_all = spread(b_ref[0, 0])
+    c_all = spread(c_ref[0, 0])
     state = jnp.where(sel_ref[places + k] == 1, r_ref[0], s_ref[0])
     for t in range(STEPS):
         u = u_ref[0, t]
@@ -25,8 +40,8 @@
         upd = jnp.dot(u_hi, expand, preferred_element_type=jnp.float32) + jnp.dot(
             u_lo, expand, preferred_element_type=jnp.float32
         )
-        state = dec_ref[0, t] * state + upd * b_ref[0, 0, t:t + 1, :]
-        prod = state * c_ref[0, 0, t:t + 1, :]
+        state = dec_ref[0, t] * state + upd * b_all[t:t + 1, :]
+        prod = state * c_all[t:t + 1, :]
         p_hi = prod.astype(jnp.bfloat16)
         p_lo = (prod - p_hi.astype(jnp.float32)).astype(jnp.bfloat16)
         dims = (((1,), (1,)), ((), ()))
@@ -43,6 +58,7 @@
     per = heads // groups
     steps = u.shape[1]
     seg = u.shape[3]
+    nsz = bt.shape[3]
     grid_spec = pltpu.PrefetchScalarGridSpec(
         num_scalar_prefetch=1,
         grid=(places, groups),
@@ -51,8 +67,8 @@
             pl.BlockSpec((1, per, cols), lambda k, g, s: (0, g, 0)),
             pl.BlockSpec((1, steps, per, seg), lambda k, g, s: (k, 0, g, 0)),
             pl.BlockSpec((1, steps, per, 1), lambda k, g, s: (k, 0, g, 0)),
-            pl.BlockSpec((1, 1, steps, cols), lambda k, g, s: (k, g, 0, 0)),
-            pl.BlockSpec((1, 1, steps, cols), lambda k, g, s: (k, g, 0, 0)),
+            pl.BlockSpec((1, 1, steps, nsz), lambda k, g, s: (k, g, 0, 0)),
+            pl.BlockSpec((1, 1, steps, nsz), lambda k, g, s: (k, g, 0, 0)),
         ],
         out_specs=[
             pl.BlockSpec((1, per, cols), lambda k, g, s: (k, g, 0)),
@@ -155,9 +171,8 @@
     heads_x = xconv.reshape(places, steps, heads_loc, head_dim)
     u = delta[..., None] * heads_x
     dec = decay[..., None]
-    reps = columns // state_size
-    bt = jnp.tile(bconv[..., :state_size], (1, 1, 1, reps)).transpose(0, 2, 1, 3)
-    ct = jnp.tile(bconv[..., state_size:], (1, 1, 1, reps)).transpose(0, 2, 1, 3)
+    bt = bconv[..., :state_size].transpose(0, 2, 1, 3)
+    ct = bconv[..., state_size:].transpose(0, 2, 1, 3)
     new_state, yk = ssm_steps(sel, ssm_state, recv, u, dec, bt, ct)
     mixed = yk + d_skip[None, None, :, None] * heads_x
     gated = mixed.reshape(places, steps, channels) * jax.nn.silu(z_in.astype(jnp.float32))

time: 98 us -> 97.8 us (level)
  local copies, waits for them, and re-layouts: 14.1 us -> 12.8 us
  Pallas kernels: 9.49 us -> 10.7 us
    another operation x4 -> x0, local copies, waits for them, and re-layouts: 1.96 us -> none  [the longest x2 0.99 us: on_device(): jnp.tile(bconv[..., state_size:], (1, 1, 1, reps)).transpose(0, 2, 1, 3)]
    pallas_call x1, Pallas kernels: 9.49 us -> 10.7 us  [ssm_steps(): pl.pallas_call(ssm_kernel, grid_spec=grid_spec, out_shape=[jax.ShapeDtype...]
where the time goes in v6:
time: 97.8 us; the launch traced here: 97.3 us
  waiting for transfers between devices  49.6 us (51%)
  local copies, waits for them, and re-layouts  12.8 us (13%)
  starting transfers between devices  11.2 us (11%)
  Pallas kernels  10.7 us (11%)
  other arithmetic  7.67 us (8%)
  between operations  2.97 us (3%)
  blocking collectives  2.45 us (3%)
    all_to_all x1, waiting for transfers between devices, migrate(): lax.all_to_all(packed, 'req', split_axis=0, concat_axis=0, tiled=True)  25.5 us
    all_to_all x1, waiting for transfers between devices, migrate(): lax.all_to_all(picked, 'req', split_axis=0, concat_axis=0, tiled=True)  24.1 us
    pallas_call x1, Pallas kernels, ssm_steps(): pl.pallas_call(ssm_kernel, grid_spec=grid_spec, out_shape=[jax.ShapeDtype...  10.7 us
    all_to_all x1, starting transfers between devices, migrate(): lax.all_to_all(packed, 'req', split_axis=0, concat_axis=0, tiled=True)  7.42 us
    all_to_all x1, starting transfers between devices, migrate(): lax.all_to_all(picked, 'req', split_axis=0, concat_axis=0, tiled=True)  3.77 us
    psum x1, blocking collectives, on_device(): total = lax.psum(jnp.sum(gated * gated, axis=-1), 'tp')  2.45 us
    select_n x1, local copies, waits for them, and re-layouts, migrate(): picked = jnp.take(spread, src_owner, axis=0)  2.12 us
  transfers between devices with their start and end apart: 2, of which 2 were waited for; matrix products, arithmetic and copies ran while one was open for 4% of the time, Pallas kernels for 0%

profile of v6, /device:TPU:0, one launch (start us, length us, event | category | flops | bytes accessed | tf_op | source)
XLA Modules:
  0.0 97.3 jit_solution(7202347591190093306)
XLA Ops:
  0.7 0.6 copy-done
  1.3 0.7 gather_fusion
  1.9 1.3 %fusion.23 = (s32[]{:T(128)}, s32[16]{0:T(128)S(1)}, pred[16]{0:T(512)(128)(4,1)S(1)}, s32[16]{0:T(128)S(1)}) fusion(s32[]{:T(128)S(6)} %axis_index.15, s32[16]{0:T(128)} %param.18, s32[16]{0:T(128)S(1)} %gather_fusion), kind=kLoop, calls=%fused_computation.121 | loop fusion | flops 655 | bytes 280 | tf_op jit(solution)/shard_map/reduce_sum | solution.py:98
  5.2 1.3 %constant_dynamic-slice_fusion = f32[1,64,4096]{2,1,0:T(8,128)S(1)} fusion(f32[2,64,4096]{2,1,0:T(8,128)} %s_ref.1, s32[]{:T(128)S(6)} %select_n.236), kind=kLoop, calls=%fused_computation.111 | loop fusion | bytes 2097156 | tf_op jit(solution)/shard_map/jit(dynamic_index_in_dim)/dynamic_slice | solution.py:106
  6.5 0.2 reshape.347
  6.7 0.5 copy-done.12
  7.3 0.2 fusion.7
  7.7 1.7 %all_to_all.14 = f32[8,1,34400]{2,1,0:T(1,128)} reshape(f32[8,34400]{1,0:T(8,128)S(1)} %pad_maximum_fusion) | data formatting | bytes 2201600 | tf_op jit(solution)/shard_map/all_to_all | solution.py:112
  9.5 7.4 %all-to-all-start = ((f32[8,1,34400]{2,1,0:T(1,128)}), f32[8,1,34400]{2,1,0:T(1,128)S(1)}, u32[]{:S(2)}, u32[]{:S(2)}) async-start(f32[8,1,34400]{2,1,0:T(1,128)} %all_to_all.14), calls=%async_computation | async-start | bytes 2203648 | tf_op jit(solution)/shard_map/all_to_all | solution.py:112
  17.1 0.2 fusion.18
  17.3 0.2 fusion.17
  17.6 0.7 broadcast_select_fusion.3
  18.3 25.5 %all-to-all-done = f32[8,1,34400]{2,1,0:T(1,128)S(1)} async-done(((f32[8,1,34400]{2,1,0:T(1,128)}), f32[8,1,34400]{2,1,0:T(1,128)S(1)}, u32[]{:S(2)}, u32[]{:S(2)}) %all-to-all-start) | async-done | bytes 1100832 | tf_op jit(solution)/shard_map/all_to_all | solution.py:112
  43.9 0.9 gather_fusion.1
  45.0 2.1 %copy.36 = f32[8,1,34400]{2,1,0:T(1,128)} copy(f32[8,1,34400]{2,0,1:T(8,128)S(1)} %bitcast_select_fusion) | data formatting | bytes 2201600 | tf_op jit(solution)/shard_map/jit(_take)/select_n | solution.py:113
  47.1 3.8 %all-to-all-start.1 = ((f32[8,1,34400]{2,1,0:T(1,128)}), f32[8,1,34400]{2,1,0:T(1,128)S(1)}, u32[]{:S(2)}, u32[]{:S(2)}) async-start(f32[8,1,34400]{2,1,0:T(1,128)} %copy.36), calls=%async_computation.1 | async-start | bytes 2203648 | tf_op jit(solution)/shard_map/all_to_all | solution.py:114
  50.9 0.9 copy.39.dec_ref
  51.8 0.6 gather_fusion.2
  52.4 0.6 pad_add_fusion.sel_ref
  53.1 0.7 broadcast_select_fusion.2
  53.8 24.1 %all-to-all-done.1 = f32[8,1,34400]{2,1,0:T(1,128)S(1)} async-done(((f32[8,1,34400]{2,1,0:T(1,128)}), f32[8,1,34400]{2,1,0:T(1,128)S(1)}, u32[]{:S(2)}, u32[]{:S(2)}) %all-to-all-start.1) | async-done | bytes 1100832 | tf_op jit(solution)/shard_map/all_to_all | solution.py:114
  78.4 1.2 %reshape.350.r_ref = f32[1,64,4096]{2,1,0:T(8,128)} reshape(f32[8,32768]{1,0:T(8,128)S(1)} %slice.103) | data formatting | bytes 2097152 | tf_op jit(solution)/shard_map/reshape | solution.py:115
  79.7 0.2 divide_multiply_fusion
  79.9 0.2 reshape.352
  80.1 0.3 slice-done
  80.5 0.7 slice_bitcast_fusion
  81.2 0.8 broadcast_multiply_fusion.u_ref
  82.0 10.7 %shard_map.192 = (f32[2,64,4096]{2,1,0:T(8,128)}, f32[2,4,64,64]{3,2,1,0:T(8,128)}) custom-call(s32[6]{0:T(128)} %pad_add_fusion.sel_ref, f32[2,64,4096]{2,1,0:T(8,128)} %s_ref.1, f32[1,64,4096]{2,1,0:T(8,128)} %reshape.350.r_ref, f32[2,4,64,64]{3,2,1,0:T(8,128)} %broadcast_multiply_fusion.u_ref, f32[2,4,64,1]{3,2,1,0:T(8,128)} %copy.39.dec_ref, ...), custom_call_target="tpu_custom_call" | custom-call | tf_op jit(solution)/shard_map/pallas_call | solution.py:78
  92.7 1.1 %multiply_add_fusion = f32[2,4,64,64]{3,2,1,0:T(8,128)S(1)} fusion(f32[2,4,64,64]{3,2,1,0:T(8,128)} %get-tuple-element.6, f32[2,4,64,64]{3,2,1,0:T(8,128)S(1)} %reshape.352, f32[64]{0:T(128)S(1)} %copy-done.15), kind=kLoop, calls=%fused_computation.7 | loop fusion | flops 65536 | bytes 393472 | tf_op jit(solution)/shard_map/add | solution.py:177
  93.9 0.2 multiply_reduce_fusion
  94.1 2.4 %psum.7 = f32[2,4]{1,0:T(2,128)S(1)} all-reduce(f32[2,4]{1,0:T(2,128)S(1)} %get-tuple-element.8), channel_id=1, replica_groups=mesh['parts'=2,'req'=8,'tp'=2] {'tp'}, use_global_device_ids=true, to_apply=%region_5.6 | all-reduce | flops 8 | bytes 64 | tf_op jit(solution)/shard_map/psum | solution.py:179
  96.6 0.7 multiply_convert_fusion
  (70 shorter events, 1.7 us)
Async XLA Ops:
  0.6 0.7 copy-start
  6.5 0.7 copy-start.12
  6.5 0.8 copy-start.3
  9.4 7.6 %copy-start.9 = (s32[16]{0:T(128)S(1)}, s32[16]{0:T(128)}, u32[]{:S(2)}) copy-start(s32[16]{0:T(128)} %param.18) | copy-start | bytes 196
  9.4 8.1 %copy-start.10 = (f32[4,2,128]{2,1,0:T(2,128)S(1)}, f32[4,2,128]{2,1,0:T(2,128)}, u32[]{:S(2)}) copy-start(f32[4,2,128]{2,1,0:T(2,128)} %param.28) | copy-start | bytes 12292
  9.4 8.1 %copy-start.16 = (f32[64]{0:T(128)S(1)}, f32[64]{0:T(128)}, u32[]{:S(2)}) copy-start(f32[64]{0:T(128)} %param.31) | copy-start | bytes 772
  9.5 8.1 %copy-start.8 = (bf16[2,4,2,128]{3,2,1,0:T(2,128)(2,1)S(1)}, bf16[2,4,2,128]{3,2,1,0:T(2,128)(2,1)}, u32[]{:S(2)}) copy-start(bf16[2,4,2,128]{3,2,1,0:T(2,128)(2,1)} %param.23) | copy-start | bytes 12292
  9.5 8.8 %copy-start.11 = (f32[2,4,64]{2,1,0:T(4,128)S(1)}, f32[2,4,64]{2,1,0:T(4,128)}, u32[]{:S(2)}) copy-start(f32[2,4,64]{2,1,0:T(4,128)} %param.25) | copy-start | bytes 6148
  9.5 8.8 %copy-start.14 = (f32[64]{0:T(128)S(1)}, f32[64]{0:T(128)}, u32[]{:S(2)}) copy-start(f32[64]{0:T(128)} %param.30) | copy-start | bytes 772
  9.5 34.3 %all-to-all-start = ((f32[8,1,34400]{2,1,0:T(1,128)}), f32[8,1,34400]{2,1,0:T(1,128)S(1)}, u32[]{:S(2)}, u32[]{:S(2)}) async-start(f32[8,1,34400]{2,1,0:T(1,128)} %all_to_all.14), calls=%async_computation | async-start | bytes 2203648 | tf_op jit(solution)/shard_map/all_to_all | solution.py:112
  47.1 4.7 %copy-start.1 = (bf16[2,4,4096]{2,1,0:T(4,128)(2,1)S(1)}, bf16[2,4,4096]{2,1,0:T(4,128)(2,1)}, u32[]{:S(2)}) copy-start(bf16[2,4,4096]{2,1,0:T(4,128)(2,1)} %param.22) | copy-start | bytes 196612
  47.1 6.7 %copy-start.5 = (f32[4,4096]{1,0:T(4,128)S(1)}, f32[4,4096]{1,0:T(4,128)}, u32[]{:S(2)}) copy-start(f32[4,4096]{1,0:T(4,128)} %param.26) | copy-start | bytes 196612
  47.1 30.9 %all-to-all-start.1 = ((f32[8,1,34400]{2,1,0:T(1,128)}), f32[8,1,34400]{2,1,0:T(1,128)S(1)}, u32[]{:S(2)}, u32[]{:S(2)}) async-start(f32[8,1,34400]{2,1,0:T(1,128)} %copy.36), calls=%async_computation.1 | async-start | bytes 2203648 | tf_op jit(solution)/shard_map/all_to_all | solution.py:114
  78.3 1.3 %copy-start.2 = (bf16[2,13056]{1,0:T(2,128)(2,1)}, bf16[2,13056]{1,0:T(2,128)(2,1)S(1)}, u32[]{:S(2)}) copy-start(bf16[2,13056]{1,0:T(2,128)(2,1)S(1)} %broadcast_select_fusion.1) | copy-start | bytes 156676
  78.4 1.3 %copy-start.6 = (f32[4096]{0:T(1024)S(1)}, f32[4096]{0:T(1024)}, u32[]{:S(2)}) copy-start(f32[4096]{0:T(1024)} %param.27) | copy-start | bytes 49156
  79.6 0.9 copy-start.13
  79.7 0.7 slice-start
  82.0 10.7 %copy-start.15 = (f32[64]{0:T(128)S(1)}, f32[64]{0:T(128)}, u32[]{:S(2)}) copy-start(f32[64]{0:T(128)} %param.32) | copy-start | bytes 772
  92.7 1.2 %copy-start.4 = (bf16[2,4,4096]{2,1,0:T(4,128)(2,1)S(1)}, bf16[2,4,4096]{2,1,0:T(4,128)(2,1)}, u32[]{:S(2)}) copy-start(bf16[2,4,4096]{2,1,0:T(4,128)(2,1)} %param.24) | copy-start | bytes 196612
  92.7 3.9 %copy-start.7 = (f32[4096]{0:T(1024)S(1)}, f32[4096]{0:T(1024)}, u32[]{:S(2)}) copy-start(f32[4096]{0:T(1024)} %param.33) | copy-start | bytes 49156
